TPU v7x, 32 devices: a whole 2x2x4 slice. The times are simulated.
32 devices in a mesh: wide: 8 (over z, x), narrow: 4 (over y, core).
Axes of the slice: x: 2, y: 2, z: 4, core: 2. Of those that a mesh axis runs over, the one named last changes fastest.
Arguments:
- tokens: bfloat16 [21504, 768], P(('wide', 'narrow')), may hold values from -6 to 6
- encoded: bfloat16 [48, 1536, 768], P(None, 'wide', 'narrow'), may hold values from -6 to 6
- lengths: int32 [48], P('wide'), may hold values from 4 to 448, as said below
- enc_frames: int32 [48], P('wide'), may hold values from 750 to 1500, as said below
- cotangent: bfloat16 [21504, 768], P(('wide', 'narrow')), may hold values from -6 to 6
- attn_gain: bfloat16 [768], replicated, may hold values from 0.099609375 to 1.8984375
- attn_shift: bfloat16 [768], replicated, may hold values from -2.5 to 2.5
- query_weight: bfloat16 [768, 768], P(None, 'narrow'), may hold values from -0.21875 to 0.21875
- query_bias: bfloat16 [768], P('narrow'), may hold values from -2.5 to 2.5
- key_weight: bfloat16 [768, 768], P(None, 'narrow'), may hold values from -0.21875 to 0.21875
- value_weight: bfloat16 [768, 768], P(None, 'narrow'), may hold values from -0.21875 to 0.21875
- value_bias: bfloat16 [768], P('narrow'), may hold values from -2.5 to 2.5
- output_weight: bfloat16 [768, 768], P('narrow'), may hold values from -1.75 to 1.75
- output_bias: bfloat16 [768], replicated, may hold values from -2.5 to 2.5
- cross_gain: bfloat16 [768], replicated, may hold values from 0.099609375 to 1.8984375
- cross_shift: bfloat16 [768], replicated, may hold values from -2.5 to 2.5
- lookup_weight: bfloat16 [768, 768], P(None, 'narrow'), may hold values from -0.21875 to 0.21875
- lookup_bias: bfloat16 [768], P('narrow'), may hold values from -2.5 to 2.5
- source_keys: bfloat16 [768, 768], P(None, 'narrow'), may hold values from -0.21875 to 0.21875
- source_values: bfloat16 [768, 768], P(None, 'narrow'), may hold values from -0.21875 to 0.21875
- source_bias: bfloat16 [768], P('narrow'), may hold values from -2.5 to 2.5
- merged_weight: bfloat16 [768, 768], P('narrow'), may hold values from -3.5 to 3.5
- merged_bias: bfloat16 [768], replicated, may hold values from -2.5 to 2.5
- dense_gain: bfloat16 [768], replicated, may hold values from 0.099609375 to 1.8984375
- dense_shift: bfloat16 [768], replicated, may hold values from -2.5 to 2.5
- expand_weight: bfloat16 [768, 3072], P(None, 'narrow'), may hold values from -0.21875 to 0.21875
- expand_bias: bfloat16 [3072], P('narrow'), may hold values from -2.5 to 2.5
- reduce_weight: bfloat16 [3072, 768], P('narrow'), may hold values from -0.109375 to 0.109375
- reduce_bias: bfloat16 [768], replicated, may hold values from -2.5 to 2.5
Outputs:
- result: bfloat16 [21504, 768], P(('wide', 'narrow'))
- tokens_grad: bfloat16 [21504, 768], P(('wide', 'narrow'))
- encoded_grad: bfloat16 [48, 1536, 768], P(None, 'wide', 'narrow')
- attn_gain_grad: float32 [768], replicated
- attn_shift_grad: float32 [768], replicated
- query_weight_grad: float32 [768, 768], P(None, 'narrow')
- query_bias_grad: float32 [768], P('narrow')
- key_weight_grad: float32 [768, 768], P(None, 'narrow')
- value_weight_grad: float32 [768, 768], P(None, 'narrow')
- value_bias_grad: float32 [768], P('narrow')
- output_weight_grad: float32 [768, 768], P('narrow')
- output_bias_grad: float32 [768], replicated
- cross_gain_grad: float32 [768], replicated
- cross_shift_grad: float32 [768], replicated
- lookup_weight_grad: float32 [768, 768], P(None, 'narrow')
- lookup_bias_grad: float32 [768], P('narrow')
- source_keys_grad: float32 [768, 768], P(None, 'narrow')
- source_values_grad: float32 [768, 768], P(None, 'narrow')
- source_bias_grad: float32 [768], P('narrow')
- merged_weight_grad: float32 [768, 768], P('narrow')
- merged_bias_grad: float32 [768], replicated
- dense_gain_grad: float32 [768], replicated
- dense_shift_grad: float32 [768], replicated
- expand_weight_grad: float32 [768, 3072], P(None, 'narrow')
- expand_bias_grad: float32 [3072], P('narrow')
- reduce_weight_grad: float32 [3072, 768], P('narrow')
- reduce_bias_grad: float32 [768], replicated
Inputs may be any that keep to these rules, and one draw needn't show every extreme that they name: Items fall into three task groups: transcription items with lengths from 224, translation items from 112, and language-id items of at most 56 positions; item 0 has 448. `enc_frames`: item 0 has 1500 live frames.
All inputs are finite; a program needn't handle non-finite values.
Results may differ from a plain program's by a relative error of at most 0.02.
Values may be sent and summed in bfloat16 or wider, within the bound.
A program may use at most 384 MiB of HBM per device.

v0:
```python
from functools import partial
from functools import reduce

import jax
import jax.numpy as jnp
from jax import lax
from jax.sharding import PartitionSpec as P

HDIM = 64
LEN = 448


def norm_forward(values, gain, shift):
    center = values - jnp.mean(values, axis=-1, keepdims=True)
    scaled = lax.rsqrt(jnp.mean(center * center, axis=-1, keepdims=True) + 1e-05)
    normal = center * scaled
    return (normal * gain.astype(jnp.float32) + shift.astype(jnp.float32), normal, scaled)


def norm_backward(grad, normal, scaled, gain):
    weighted = grad * gain.astype(jnp.float32)
    centered = weighted - jnp.mean(weighted, axis=-1, keepdims=True)
    return scaled * (centered - normal * jnp.mean(weighted * normal, axis=-1, keepdims=True))


def head_view(values):
    return values.reshape(values.shape[0], values.shape[1], values.shape[2] // HDIM, HDIM)


def attention_scores(query, keys, allowed):
    raw = jnp.einsum(
        "blhe,bshe->bhls", head_view(query), head_view(keys), preferred_element_type=jnp.float32
    )
    return jnp.where(allowed, raw * HDIM ** (-0.5), -1e30)


def attention_forward(query, keys, values, allowed):
    scores = attention_scores(query, keys, allowed)
    largest = jnp.max(scores, axis=-1, keepdims=True)
    expos = jnp.exp(scores - largest)
    totals = jnp.sum(expos, axis=-1, keepdims=True)
    probs = (expos / totals).astype(jnp.bfloat16)
    mixed = jnp.einsum(
        "bhls,bshe->blhe", probs, head_view(values), preferred_element_type=jnp.float32
    )
    return (mixed.reshape(query.shape).astype(jnp.bfloat16), largest, totals)


def attention_backward(query, keys, values, allowed, largest, totals, grad_out):
    scores = attention_scores(query, keys, allowed)
    probs = jnp.exp(scores - largest) / totals
    grads = head_view(grad_out)
    dprobs = jnp.einsum(
        "blhe,bshe->bhls", grads, head_view(values), preferred_element_type=jnp.float32
    )
    dscores = (probs * (dprobs - jnp.sum(probs * dprobs, axis=-1, keepdims=True))).astype(
        jnp.bfloat16
    )
    scale = HDIM ** (-0.5)
    dquery = (
        jnp.einsum("bhls,bshe->blhe", dscores, head_view(keys), preferred_element_type=jnp.float32)
        * scale
    )
    dkeys = (
        jnp.einsum("bhls,blhe->bshe", dscores, head_view(query), preferred_element_type=jnp.float32)
        * scale
    )
    dvalues = jnp.einsum(
        "bhls,blhe->bshe", probs.astype(jnp.bfloat16), grads, preferred_element_type=jnp.float32
    )
    return (
        dquery.reshape(query.shape).astype(jnp.bfloat16),
        dkeys.reshape(keys.shape).astype(jnp.bfloat16),
        dvalues.reshape(values.shape).astype(jnp.bfloat16),
    )


def project(inputs, weight, bias):
    return jnp.dot(inputs, weight, preferred_element_type=jnp.float32) + bias.astype(jnp.float32)


def weight_grad(inputs, grads):
    return jnp.einsum("rk,rd->kd", inputs, grads, preferred_element_type=jnp.float32)


def on_device(
    tokens,
    encoded,
    lengths,
    enc_frames,
    cotangent,
    attn_gain,
    attn_shift,
    query_weight,
    query_bias,
    key_weight,
    value_weight,
    value_bias,
    output_weight,
    output_bias,
    cross_gain,
    cross_shift,
    lookup_weight,
    lookup_bias,
    source_keys,
    source_values,
    source_bias,
    merged_weight,
    merged_bias,
    dense_gain,
    dense_shift,
    expand_weight,
    expand_bias,
    reduce_weight,
    reduce_bias,
):
    local = tokens.shape[0]
    items = lengths.shape[0]
    total_rows = items * LEN

    def gather_rows(values):
        return lax.all_gather(values.astype(jnp.bfloat16), "narrow", axis=0, tiled=True)

    def gather_grads(values):
        return lax.all_gather(values.astype(jnp.bfloat16), "narrow", axis=0, tiled=True)

    def branch_sum(inputs, weight):
        piece = lax.dynamic_slice_in_dim(inputs, jnp.int32(0), lax.axis_size("narrow") * local, 0)
        return lax.psum_scatter(
            jnp.dot(piece, weight, preferred_element_type=jnp.float32),
            "narrow",
            scatter_dimension=0,
            tiled=True,
        )

    def input_sum(pairs):
        parts = [
            jnp.einsum("rk,dk->rd", grad, weight, preferred_element_type=jnp.float32)
            for grad, weight in pairs
        ]
        return lax.psum_scatter(reduce(jnp.add, parts), "narrow", scatter_dimension=0, tiled=True)

    regrouped = lax.all_to_all(encoded, "wide", split_axis=0, concat_axis=1, tiled=True)
    source = lax.all_gather(regrouped, "narrow", axis=2, tiled=True)
    frames = source.shape[1]
    places = jnp.arange(LEN)
    causal = (places[None, :] <= places[:, None])[None, None] & (
        places[None, None, None, :] < lengths[:, None, None, None]
    )
    heard = jnp.arange(frames)[None, None, None, :] < enc_frames[:, None, None, None]
    rows_in = tokens.astype(jnp.float32)
    normed_self, normal_self, scaled_self = norm_forward(rows_in, attn_gain, attn_shift)
    first = gather_rows(normed_self)
    query = project(first, query_weight, query_bias).astype(jnp.bfloat16).reshape(items, LEN, -1)
    keys = (
        jnp.dot(first, key_weight, preferred_element_type=jnp.float32)
        .astype(jnp.bfloat16)
        .reshape(items, LEN, -1)
    )
    values = project(first, value_weight, value_bias).astype(jnp.bfloat16).reshape(items, LEN, -1)
    attended, top_self, total_self = attention_forward(query, keys, values, causal)
    attended = attended.reshape(total_rows, -1)
    after_self = rows_in + branch_sum(attended, output_weight) + output_bias.astype(jnp.float32)
    normed_cross, normal_cross, scaled_cross = norm_forward(after_self, cross_gain, cross_shift)
    second = gather_rows(normed_cross)
    lookup = (
        project(second, lookup_weight, lookup_bias).astype(jnp.bfloat16).reshape(items, LEN, -1)
    )
    heard_keys = jnp.einsum(
        "bsd,dk->bsk", source, source_keys, preferred_element_type=jnp.float32
    ).astype(jnp.bfloat16)
    heard_values = (
        jnp.einsum("bsd,dk->bsk", source, source_values, preferred_element_type=jnp.float32)
        + source_bias.astype(jnp.float32)
    ).astype(jnp.bfloat16)
    recalled, top_cross, total_cross = attention_forward(lookup, heard_keys, heard_values, heard)
    recalled = recalled.reshape(total_rows, -1)
    after_cross = after_self + branch_sum(recalled, merged_weight) + merged_bias.astype(jnp.float32)
    normed_dense, normal_dense, scaled_dense = norm_forward(after_cross, dense_gain, dense_shift)
    third = gather_rows(normed_dense)
    widened = project(third, expand_weight, expand_bias)
    active = partial(jax.nn.gelu, approximate=False)
    activated = active(widened).astype(jnp.bfloat16)
    result = (
        after_cross + branch_sum(activated, reduce_weight) + reduce_bias.astype(jnp.float32)
    ).astype(jnp.bfloat16)
    grad_out = cotangent.astype(jnp.float32)
    grad_reduce_bias = jnp.sum(grad_out, axis=0)
    spread_dense = gather_grads(cotangent)
    grad_reduce = weight_grad(activated, spread_dense)
    grad_active = jnp.einsum(
        "rd,fd->rf", spread_dense, reduce_weight, preferred_element_type=jnp.float32
    )
    unused, pull = jax.vjp(active, widened)
    grad_widened = pull(grad_active)[0].astype(jnp.bfloat16)
    grad_expand_bias = jnp.sum(grad_widened.astype(jnp.float32), axis=0)
    grad_expand = weight_grad(third, grad_widened)
    back_dense = input_sum(((grad_widened, expand_weight),))
    grad_dense_gain = jnp.sum(back_dense * normal_dense, axis=0)
    grad_dense_shift = jnp.sum(back_dense, axis=0)
    grad_after_cross = grad_out + norm_backward(back_dense, normal_dense, scaled_dense, dense_gain)
    grad_merged_bias = jnp.sum(grad_after_cross, axis=0)
    spread_cross = gather_grads(grad_after_cross)
    grad_merged = weight_grad(recalled, spread_cross)
    grad_recalled = (
        jnp.einsum("rd,kd->rk", spread_cross, merged_weight, preferred_element_type=jnp.float32)
        .astype(jnp.bfloat16)
        .reshape(items, LEN, -1)
    )
    d_lookup, d_heard_keys, d_heard_values = attention_backward(
        lookup, heard_keys, heard_values, heard, top_cross, total_cross, grad_recalled
    )
    d_lookup = d_lookup.reshape(total_rows, -1)
    grad_lookup_bias = jnp.sum(d_lookup.astype(jnp.float32), axis=0)
    grad_lookup = weight_grad(second, d_lookup)
    grad_source_keys = jnp.einsum(
        "bsd,bsk->dk", source, d_heard_keys, preferred_element_type=jnp.float32
    )
    grad_source_values = jnp.einsum(
        "bsd,bsk->dk", source, d_heard_values, preferred_element_type=jnp.float32
    )
    grad_source_bias = jnp.sum(d_heard_values.astype(jnp.float32), axis=(0, 1))
    source_part = jnp.einsum(
        "bsk,dk->bsd", d_heard_keys, source_keys, preferred_element_type=jnp.float32
    ) + jnp.einsum("bsk,dk->bsd", d_heard_values, source_values, preferred_element_type=jnp.float32)
    source_share = lax.psum_scatter(source_part, "narrow", scatter_dimension=2, tiled=True)
    encoded_grad = lax.all_to_all(
        source_share.astype(jnp.bfloat16), "wide", split_axis=1, concat_axis=0, tiled=True
    )
    back_cross = input_sum(((d_lookup, lookup_weight),))
    grad_cross_gain = jnp.sum(back_cross * normal_cross, axis=0)
    grad_cross_shift = jnp.sum(back_cross, axis=0)
    grad_after_self = grad_after_cross + norm_backward(
        back_cross, normal_cross, scaled_cross, cross_gain
    )
    grad_output_bias = jnp.sum(grad_after_self, axis=0)
    spread_self = gather_grads(grad_after_self)
    grad_output = weight_grad(attended, spread_self)
    grad_attended = (
        jnp.einsum("rd,kd->rk", spread_self, output_weight, preferred_element_type=jnp.float32)
        .astype(jnp.bfloat16)
        .reshape(items, LEN, -1)
    )
    d_query, d_keys, d_values = attention_backward(
        query, keys, values, causal, top_self, total_self, grad_attended
    )
    d_query = d_query.reshape(total_rows, -1)
    d_keys = d_keys.reshape(total_rows, -1)
    d_values = d_values.reshape(total_rows, -1)
    grad_query_bias = jnp.sum(d_query.astype(jnp.float32), axis=0)
    grad_value_bias = jnp.sum(d_values.astype(jnp.float32), axis=0)
    grad_query = weight_grad(first, d_query)
    grad_key = weight_grad(first, d_keys)
    grad_value = weight_grad(first, d_values)
    back_self = input_sum(((d_query, query_weight), (d_keys, key_weight), (d_values, value_weight)))
    grad_attn_gain = jnp.sum(back_self * normal_self, axis=0)
    grad_attn_shift = jnp.sum(back_self, axis=0)
    tokens_grad = (
        grad_after_self + norm_backward(back_self, normal_self, scaled_self, attn_gain)
    ).astype(jnp.bfloat16)
    small = lax.psum(
        (
            grad_attn_gain,
            grad_attn_shift,
            grad_output_bias,
            grad_cross_gain,
            grad_cross_shift,
            grad_merged_bias,
            grad_dense_gain,
            grad_dense_shift,
            grad_reduce_bias,
        ),
        "narrow",
    )
    summed_all = lax.psum(
        (
            grad_query,
            grad_query_bias,
            grad_key,
            grad_value,
            grad_value_bias,
            grad_output,
            small[0],
            small[1],
            small[2],
            small[3],
            small[4],
            small[5],
            small[6],
            small[7],
            small[8],
            grad_expand,
            grad_expand_bias,
            grad_reduce,
            grad_lookup,
            grad_lookup_bias,
            grad_source_keys,
            grad_source_values,
            grad_source_bias,
            grad_merged,
        ),
        "wide",
    )
    (
        sum_query,
        sum_query_bias,
        sum_key,
        sum_value,
        sum_value_bias,
        sum_output,
        sum_attn_gain,
        sum_attn_shift,
        sum_output_bias,
        sum_cross_gain,
        sum_cross_shift,
        sum_merged_bias,
        sum_dense_gain,
        sum_dense_shift,
        sum_reduce_bias,
        sum_expand,
        sum_expand_bias,
        sum_reduce,
        sum_lookup,
        sum_lookup_bias,
        sum_source_keys,
        sum_source_values,
        sum_source_bias,
        sum_merged,
    ) = summed_all
    return (
        result,
        tokens_grad,
        encoded_grad,
        sum_attn_gain,
        sum_attn_shift,
        sum_query,
        sum_query_bias,
        sum_key,
        sum_value,
        sum_value_bias,
        sum_output,
        sum_output_bias,
        sum_cross_gain,
        sum_cross_shift,
        sum_lookup,
        sum_lookup_bias,
        sum_source_keys,
        sum_source_values,
        sum_source_bias,
        sum_merged,
        sum_merged_bias,
        sum_dense_gain,
        sum_dense_shift,
        sum_expand,
        sum_expand_bias,
        sum_reduce,
        sum_reduce_bias,
    )


def solution(mesh):
    placed = (
        P(("wide", "narrow"), None),
        P(None, "wide", "narrow"),
        P("wide"),
        P("wide"),
        P(("wide", "narrow"), None),
        P(),
        P(),
        P(None, "narrow"),
        P("narrow"),
        P(None, "narrow"),
        P(None, "narrow"),
        P("narrow"),
        P("narrow", None),
        P(),
        P(),
        P(),
        P(None, "narrow"),
        P("narrow"),
        P(None, "narrow"),
        P(None, "narrow"),
        P("narrow"),
        P("narrow", None),
        P(),
        P(),
        P(),
        P(None, "narrow"),
        P("narrow"),
        P("narrow", None),
        P(),
    )
    return jax.shard_map(
        on_device,
        mesh=mesh,
        in_specs=placed,
        out_specs=(
            P(("wide", "narrow"), None),
            P(("wide", "narrow"), None),
            P(None, "wide", "narrow"),
            P(),
            P(),
            P(None, "narrow"),
            P("narrow"),
            P(None, "narrow"),
            P(None, "narrow"),
            P("narrow"),
            P("narrow", None),
            P(),
            P(),
            P(),
            P(None, "narrow"),
            P("narrow"),
            P(None, "narrow"),
            P(None, "narrow"),
            P("narrow"),
            P("narrow", None),
            P(),
            P(),
            P(),
            P(None, "narrow"),
            P("narrow"),
            P("narrow", None),
            P(),
        ),
        check_vma=False,
    )
```

profile of v0, /device:TPU:0, one launch (start us, length us, event | category | flops | bytes accessed | tf_op | source)
XLA Modules:
  0.0 1737.9 jit_solution(3418779017324385512)
XLA Ops:
  17.1 35.1 %all-gather.8.cloned.1.call-done = bf16[2688,768]{1,0:T(8,128)(2,1)} async-done(((bf16[672,768]{1,0:T(8,128)(2,1)}), bf16[2688,768]{1,0:T(8,128)(2,1)}) %all-gather.8.cloned.1.call-update) | async-done | bytes 4128784 | tf_op jit(solution)/shard_map/all_gather | solution.py:122
  78.0 14.6 fusion.103
  92.6 7.8 fusion.61
  109.7 110.4 %all_to_all.36 = bf16[48,192,192]{2,1,0:T(8,128)(2,1)} all-to-all(bf16[48,192,192]{2,1,0:T(8,128)(2,1)} %param.30), channel_id=1, replica_groups=mesh['wide'=8,'narrow'=4] {'wide'}, dimensions={0} | all-to-all | bytes 7077888 | tf_op jit(solution)/shard_map/all_to_all | solution.py:143
  220.1 7.6 copy.103
  227.8 8.2 all_to_all.29
  243.0 82.3 %all-gather.10.cloned.1.call-done = bf16[6,1536,768]{1,2,0:T(8,128)(2,1)} async-done(((bf16[6,1536,192]{1,2,0:T(8,128)(2,1)}), bf16[6,1536,768]{1,2,0:T(8,128)(2,1)}) %all-gather.10.cloned.1.call-update) | async-done | bytes 14155792 | tf_op jit(solution)/shard_map/all_gather | solution.py:144
  325.3 9.9 convolution_convert_fusion
  335.6 12.9 add_convert_fusion.1
  348.5 13.0 all-gather.12.cloned.1.call-done
  370.1 21.0 %fusion.71 = f32[6,3,448,1536]{3,2,1,0:T(8,128)} fusion(bf16[6,1536,3,64]{1,3,2,0:T(8,128)(2,1)} %bitcast.133, bf16[6,448,3,64]{1,0,3,2:T(8,128)(2,1)} %reshape_reshape.28), kind=kOutput, calls=%fused_computation.123 | convolution fusion | flops 1585446912 | bytes 54116352 | tf_op jit(solution)/shard_map/blhe,bshe->bhls/dot_general | solution.py:31
  391.1 52.4 %fusion.112 = (f32[6,3,448]{2,1,0:T(4,128)S(1)}, f32[6,3,448,1536]{3,2,1,0:T(8,128)}) fusion(f32[6,3,448,1536]{3,2,1,0:T(8,128)} %fusion.71, pred[6,1536]{1,0:T(8,128)(4,1)S(1)} %iota_compare_fusion.1), kind=kOutput, calls=%fused_computation.162 | output fusion | flops 74319360 | bytes 99131904 | tf_op jit(solution)/shard_map/sub | solution.py:40
  444.1 20.1 %fusion.57 = bf16[6,448,3,64]{1,3,2,0:T(8,128)(2,1)} fusion(bf16[6,1536,3,64]{1,3,2,0:T(8,128)(2,1)} %bitcast.145, f32[6,3,448,1536]{3,2,1,0:T(8,128)} %get-tuple-element.88, f32[6,3,448]{2,1,0:T(4,128)S(1)} %get-tuple-element.87), kind=kOutput, calls=%fused_computation.110 | convolution fusion | flops 1610735616 | bytes 54148608 | tf_op jit(solution)/shard_map/bhls,bshe->blhe/dot_general | solution.py:43
  471.1 5.7 fusion.114
  478.2 69.7 %reduce-scatter.10.cloned.1.call-done = f32[672,768]{1,0:T(8,128)} async-done(((f32[2688,768]{1,0:T(8,128)}), f32[672,768]{1,0:T(8,128)}) %reduce-scatter.10.cloned.1.call-update) | async-done | bytes 2064400 | tf_op jit(solution)/shard_map/reduce_scatter | solution.py:129
  553.3 33.5 %all-gather.14.cloned.1.call-done = bf16[2688,768]{1,0:T(8,128)(2,1)} async-done(((bf16[672,768]{1,0:T(8,128)(2,1)}), bf16[2688,768]{1,0:T(8,128)(2,1)}) %all-gather.14.cloned.1.call-update) | async-done | bytes 4128784 | tf_op jit(solution)/shard_map/all_gather | solution.py:122
  586.8 9.4 fusion.115
  596.1 26.3 %all-gather.16.cloned.1.call-done = bf16[2688,768]{1,0:T(8,128)(2,1)} async-done(((bf16[672,768]{1,0:T(8,128)(2,1)}), bf16[2688,768]{1,0:T(8,128)(2,1)}) %all-gather.16.cloned.1.call-update) | async-done | bytes 4128784 | tf_op jit(solution)/shard_map/all_gather | solution.py:125
  622.5 25.3 %convert_reduce_fusion = (f32[768]{0:T(1024)}, bf16[2688,768]{1,0:T(8,128)(2,1)S(1)}, f32[2688,768]{1,0:T(8,128)}) fusion(f32[2688,768]{1,0:T(8,128)} %fusion.115, f32[768]{0:T(1024)S(1)} %convert_element_type.258, bf16[2688,768]{1,0:T(8,128)(2,1)} %all-gather.16.cloned.1.call-done, bf16[768,768]{1,0:T(8,128)(2,1)S(1)} %copy-done), kind=kOutput, calls=%fused_computation.23 | convolution fusion | flops 3325721856 | bytes 25958400 | tf_op jit(solution)/shard_map/rd,fd->rf/dot_general | solution.py:191
  649.8 5.5 fusion.117
  655.4 7.1 multiply_convert_fusion.2
  665.1 5.9 fusion.116
  671.7 54.8 %reduce-scatter.14.cloned.1.call-done = f32[672,768]{1,0:T(8,128)} async-done(((f32[2688,768]{1,0:T(8,128)}), f32[672,768]{1,0:T(8,128)}) %reduce-scatter.14.cloned.1.call-update) | async-done | bytes 2064400 | tf_op jit(solution)/shard_map/reduce_scatter | solution.py:141
  729.5 70.5 %reduce-scatter.12.cloned.1.call-done = f32[672,768]{1,0:T(8,128)} async-done(((f32[2688,768]{1,0:T(8,128)}), f32[672,768]{1,0:T(8,128)}) %reduce-scatter.12.cloned.1.call-update) | async-done | bytes 2064400 | tf_op jit(solution)/shard_map/reduce_scatter | solution.py:129
  806.5 34.2 %all-gather.18.cloned.1.call-done = bf16[2688,768]{1,0:T(8,128)(2,1)} async-done(((bf16[672,768]{1,0:T(8,128)(2,1)}), bf16[2688,768]{1,0:T(8,128)(2,1)}) %all-gather.18.cloned.1.call-update) | async-done | bytes 4128784 | tf_op jit(solution)/shard_map/all_gather | solution.py:125
  846.4 34.8 %multiply_reduce_fusion = (f32[6,3,448]{2,1,0:T(4,128)S(1)}, f32[6,3,448,1536]{3,2,1,0:T(8,128)}) fusion(f32[6,3,448,1536]{3,2,1,0:T(8,128)} %get-tuple-element.88, f32[6,3,448]{2,1,0:T(4,128)S(1)} %copy-done.69, bf16[6,1536,3,64]{1,3,2,0:T(8,128)(2,1)} %bitcast.146, bf16[6,448,3,64]{1,0,3,2:T(8,128)(2,1)S(1)} %reshape_reshape.29), kind=kOutput, calls=%fused_computation.3 | convolution fusion | flops 1622597760 | bytes 103726080 | tf_op jit(solution)/shard_map/blhe,bshe->bhls/dot_general | solution.py:53
  881.3 39.5 %multiply_convert_fusion = bf16[6,3,448,1536]{3,2,1,0:T(8,128)(2,1)} fusion(f32[6,3,448,1536]{3,2,1,0:T(8,128)} %get-tuple-element.90, f32[6,3,448]{2,1,0:T(4,128)S(1)} %get-tuple-element.89, f32[6,3,448,1536]{3,2,1,0:T(8,128)} %get-tuple-element.88, f32[6,3,448]{2,1,0:T(4,128)S(1)} %copy-done.69), kind=kLoop, calls=%fused_computation.2 | loop fusion | flops 49545216 | bytes 123927552 | tf_op jit(solution)/shard_map/convert_element_type | solution.py:56
  920.8 13.5 convert_reduce_fusion.4
  942.6 15.1 multiply_convert_fusion.3
  959.5 11.9 fusion.88
  971.4 40.9 %reduce-scatter.16.cloned.1.call-done = f32[672,768]{1,0:T(8,128)} async-done(((f32[2688,768]{1,0:T(8,128)}), f32[672,768]{1,0:T(8,128)}) %reduce-scatter.16.cloned.1.call-update) | async-done | bytes 2064400 | tf_op jit(solution)/shard_map/reduce_scatter | solution.py:141
  1019.4 21.0 %convert_reduce_fusion.1 = (f32[3,64]{1,0:T(4,128)}, bf16[6,3,64,1536]{3,2,1,0:T(8,128)(2,1)}) fusion(f32[6,3,448,1536]{3,2,1,0:T(8,128)} %get-tuple-element.88, f32[6,3,448]{2,1,0:T(4,128)S(1)} %copy-done.70, bf16[6,448,3,64]{1,0,3,2:T(8,128)(2,1)S(1)} %copy-done.35), kind=kOutput, calls=%fused_computation.44 | convolution fusion | flops 1615527680 | bytes 54149376 | tf_op jit(solution)/shard_map/bhls,blhe->bshe/dot_general | solution.py:68
  1040.4 19.1 %convolution_add_fusion = f32[6,1536,768]{1,2,0:T(8,128)} fusion(f32[6,1536,768]{1,2,0:T(8,128)} %fusion.88, bf16[6,1536,192]{1,2,0:T(8,128)(2,1)} %bitcast.139, bf16[768,192]{0,1:T(8,128)(2,1)S(1)} %copy-done.44), kind=kOutput, calls=%fused_computation.11 | convolution fusion | flops 2724986880 | bytes 60456960 | tf_op jit(solution)/shard_map/bsk,dk->bsd/dot_general | solution.py:225
  1066.0 12.4 convert_reduce_fusion.5
  1080.6 19.2 %multiply_reduce_fusion.1 = (f32[6,3,448]{2,1,0:T(4,128)S(1)}, f32[6,3,448,448]{2,3,1,0:T(8,128)}) fusion(f32[6,3,448,448]{2,3,1,0:T(8,128)} %get-tuple-element.86, f32[6,3,448]{2,1,0:T(4,128)S(1)} %copy-done.72, bf16[6,448,3,64]{1,0,3,2:T(8,128)(2,1)} %reshape_reshape.12, bf16[6,448,3,64]{1,0,3,2:T(8,128)(2,1)} %copy-done.36), kind=kOutput, calls=%fused_computation.13 | convolution fusion | flops 473251968 | bytes 31030272 | tf_op jit(solution)/shard_map/blhe,bshe->bhls/dot_general | solution.py:53
  1099.8 12.7 multiply_convert_fusion.1
  1120.8 6.3 fusion.60
  1139.4 8.6 fusion.123
  1157.7 11.8 convolution_bitcast_fusion
  1169.4 9.0 convolution_bitcast_fusion.1
  1188.2 72.5 %reduce-scatter.20.cloned.1.call-done = f32[6,1536,192]{1,2,0:T(8,128)} async-done(((f32[6,1536,768]{1,2,0:T(8,128)}), f32[6,1536,192]{1,2,0:T(8,128)}) %reduce-scatter.20.cloned.1.call-update) | async-done | bytes 7077904 | tf_op jit(solution)/shard_map/reduce_scatter | solution.py:226
  1265.9 8.8 copy.121
  1274.8 5.5 all-to-all-start.1
  1280.7 53.6 %reduce-scatter.18.cloned.1.call-done = f32[672,768]{1,0:T(8,128)} async-done(((f32[2688,768]{1,0:T(8,128)}), f32[672,768]{1,0:T(8,128)}) %reduce-scatter.18.cloned.1.call-update) | async-done | bytes 2064400 | tf_op jit(solution)/shard_map/reduce_scatter | solution.py:141
  1336.9 11.3 all-reduce.2
  1348.2 186.8 %all-reduce = (f32[768]{0:T(1024)}, f32[768]{0:T(1024)}, f32[192]{0:T(256)}, f32[192]{0:T(256)}, f32[768]{0:T(1024)}, /*index=5*/f32[768]{0:T(1024)}, f32[768]{0...) all-reduce(f32[768]{0:T(1024)S(1)} %get-tuple-element.63, ...), channel_id=1, replica_groups=mesh['wide'=8,'narrow'=4] {'wide'}, use_global_device_ids=true, to_apply=%region_27.28 | all-reduce | flops 8448 | bytes 67584 | tf_op jit(solution)/shard_map/psum | solution.py:275
  1538.3 6.2 copy.122
  1544.6 172.3 %all-reduce.5.cloned.1.call-done = (f32[768,192]{0,1:T(8,128)}, f32[768,192]{0,1:T(8,128)}, f32[768,192]{0,1:T(8,128)}, f32[192,768]{1,0:T(8,128)}, f32[768,192]...) async-done(((f32[768,192]{0,1:T(8,128)}, f32[768,192]{0,1:T(8,128)}, ...) | async-done | bytes 9437200 | tf_op jit(solution)/shard_map/psum | solution.py:275
  (331 shorter events, 186.3 us)
Async XLA Ops:
  7.2 615.3 %copy-start = (bf16[768,768]{1,0:T(8,128)(2,1)S(1)}, bf16[768,768]{1,0:T(8,128)(2,1)}, u32[]{:S(2)}) copy-start(bf16[768,768]{1,0:T(8,128)(2,1)} %param.56) | copy-start | bytes 3538948
  7.3 44.9 %copy-start.50 = (bf16[768,192]{0,1:T(8,128)(2,1)S(1)}, bf16[768,192]{0,1:T(8,128)(2,1)}, u32[]{:S(2)}) copy-start(bf16[768,192]{0,1:T(8,128)(2,1)} %param.36) | copy-start | bytes 884740
  7.3 44.9 %all-gather.8.cloned.1.call-start = ((), (), s32[]{:S(2)}) async-start(), calls=%async_computation.9 | async-start | bytes 5160960 | tf_op jit(solution)/shard_map/all_gather | solution.py:122
  15.2 221.0 %reduce-scatter.8.cloned.1.call-start = ((), (), s32[]{:S(2)}) async-start(), calls=%async_computation.10 | async-start | bytes 10321920 | tf_op jit(solution)/shard_map/reduce_scatter | solution.py:129
  17.1 42.8 %copy-start.54 = (bf16[768,192]{0,1:T(8,128)(2,1)S(1)}, bf16[768,192]{0,1:T(8,128)(2,1)}, u32[]{:S(2)}) copy-start(bf16[768,192]{0,1:T(8,128)(2,1)} %param.39) | copy-start | bytes 884740
  109.7 215.6 %all-gather.10.cloned.1.call-start = ((), (), s32[]{:S(2)}) async-start(), calls=%async_computation.11 | async-start | bytes 17694720 | tf_op jit(solution)/shard_map/all_gather | solution.py:144
  236.0 125.5 %all-gather.12.cloned.1.call-start = ((), (), s32[]{:S(2)}) async-start(), calls=%async_computation.12 | async-start | bytes 5160960 | tf_op jit(solution)/shard_map/all_gather | solution.py:122
  238.3 309.6 %copy-start.2 = (f32[672,768]{1,0:T(8,128)}, f32[672,768]{1,0:T(8,128)S(1)}, u32[]{:S(2)}) copy-start(f32[672,768]{1,0:T(8,128)S(1)} %get-tuple-element.82) | copy-start | bytes 6193156
  238.4 87.0 %copy-start.37 = (bf16[768,192]{0,1:T(8,128)(2,1)S(1)}, bf16[768,192]{0,1:T(8,128)(2,1)}, u32[]{:S(2)}) copy-start(bf16[768,192]{0,1:T(8,128)(2,1)} %param.47) | copy-start | bytes 884740
  241.1 306.8 %reduce-scatter.10.cloned.1.call-start = ((), (), s32[]{:S(2)}) async-start(), calls=%async_computation.13 | async-start | bytes 10321920 | tf_op jit(solution)/shard_map/reduce_scatter | solution.py:129
  335.6 25.9 %copy-start.46 = (bf16[768,192]{0,1:T(8,128)(2,1)S(1)}, bf16[768,192]{0,1:T(8,128)(2,1)}, u32[]{:S(2)}) copy-start(bf16[768,192]{0,1:T(8,128)(2,1)} %param.45) | copy-start | bytes 884740
  335.6 25.9 %copy-start.97 = (f32[192]{0:T(256)S(1)}, f32[192]{0:T(256)}, u32[]{:S(2)}) copy-start(f32[192]{0:T(256)} %convert_element_type.247) | copy-start | bytes 2308
  476.9 109.9 %all-gather.14.cloned.1.call-start = ((), (), s32[]{:S(2)}) async-start(), calls=%async_computation.14 | async-start | bytes 5160960 | tf_op jit(solution)/shard_map/all_gather | solution.py:122
  552.5 70.0 %all-gather.16.cloned.1.call-start = ((), (), s32[]{:S(2)}) async-start(), calls=%async_computation.16 | async-start | bytes 5160960 | tf_op jit(solution)/shard_map/all_gather | solution.py:125
  553.2 173.2 %reduce-scatter.14.cloned.1.call-start = ((), (), s32[]{:S(2)}) async-start(), calls=%async_computation.17 | async-start | bytes 10321920 | tf_op jit(solution)/shard_map/reduce_scatter | solution.py:141
  622.5 27.3 %copy-start.93 = (bf16[768,768]{1,0:T(8,128)(2,1)S(1)}, bf16[768,768]{1,0:T(8,128)(2,1)}, u32[]{:S(2)}) copy-start(bf16[768,768]{1,0:T(8,128)(2,1)} %param.54) | copy-start | bytes 3538948
  655.4 144.6 %reduce-scatter.12.cloned.1.call-start = ((), (), s32[]{:S(2)}) async-start(), calls=%async_computation.15 | async-start | bytes 10321920 | tf_op jit(solution)/shard_map/reduce_scatter | solution.py:129
  671.0 55.4 %copy-start.6 = (f32[672,768]{1,0:T(8,128)S(1)}, f32[672,768]{1,0:T(8,128)}, u32[]{:S(2)}) copy-start(f32[672,768]{1,0:T(8,128)} %copy-done.5) | copy-start | bytes 6193156
  671.0 129.0 %copy-start.27 = (bf16[672,768]{1,0:T(8,128)(2,1)S(1)}, bf16[672,768]{1,0:T(8,128)(2,1)}, u32[]{:S(2)}) copy-start(bf16[672,768]{1,0:T(8,128)(2,1)} %param.33) | copy-start | bytes 3096580
  671.0 169.7 %all-gather.18.cloned.1.call-start = ((), (), s32[]{:S(2)}) async-start(), calls=%async_computation.18 | async-start | bytes 5160960 | tf_op jit(solution)/shard_map/all_gather | solution.py:125
  806.5 39.9 %copy-start.69 = (f32[6,3,448]{2,1,0:T(4,128)S(1)}, f32[6,3,448]{2,1,0:T(4,128)}, u32[]{:S(2)}) copy-start(f32[6,3,448]{2,1,0:T(4,128)} %copy-done.68) | copy-start | bytes 96772
  806.5 205.8 %reduce-scatter.16.cloned.1.call-start = ((), (), s32[]{:S(2)}) async-start(), calls=%async_computation.19 | async-start | bytes 10321920 | tf_op jit(solution)/shard_map/reduce_scatter | solution.py:141
  846.4 34.9 %copy-start.34 = (bf16[6,448,3,64]{1,0,3,2:T(8,128)(2,1)}, bf16[6,448,3,64]{1,0,3,2:T(8,128)(2,1)S(1)}, u32[]{:S(2)}) copy-start(bf16[6,448,3,64]{1,0,3,2:T(8,128)(2,1)S(1)} %reshape_reshape.29) | copy-start | bytes 3096580
  941.2 18.3 %copy-start.38 = (bf16[768,192]{0,1:T(8,128)(2,1)S(1)}, bf16[768,192]{0,1:T(8,128)(2,1)}, u32[]{:S(2)}) copy-start(bf16[768,192]{0,1:T(8,128)(2,1)} %param.47) | copy-start | bytes 884740
  941.2 118.8 %all-gather.20.cloned.1.call-start = ((), (), s32[]{:S(2)}) async-start(), calls=%async_computation.20 | async-start | bytes 5160960 | tf_op jit(solution)/shard_map/all_gather | solution.py:125
  959.5 52.7 %copy-start.3 = (f32[672,768]{1,0:T(8,128)S(1)}, f32[672,768]{1,0:T(8,128)}, u32[]{:S(2)}) copy-start(f32[672,768]{1,0:T(8,128)} %copy-done.2) | copy-start | bytes 6193156
  959.5 52.7 %copy-start.57 = (f32[672]{0:T(1024)S(1)}, f32[672]{0:T(1024)}, u32[]{:S(2)}) copy-start(f32[672]{0:T(1024)} %copy-done.56) | copy-start | bytes 8068
  959.5 52.7 %copy-start.61 = (f32[768]{0:T(1024)S(1)}, f32[768]{0:T(1024)}, u32[]{:S(2)}) copy-start(f32[768]{0:T(1024)} %copy-done.60) | copy-start | bytes 9220
  959.5 52.7 %copy-start.63 = (f32[672]{0:T(1024)S(1)}, f32[672]{0:T(1024)}, u32[]{:S(2)}) copy-start(f32[672]{0:T(1024)} %copy-done.62) | copy-start | bytes 8068
  1019.3 21.1 %copy-start.44 = (bf16[768,192]{0,1:T(8,128)(2,1)S(1)}, bf16[768,192]{0,1:T(8,128)(2,1)}, u32[]{:S(2)}) copy-start(bf16[768,192]{0,1:T(8,128)(2,1)} %param.48) | copy-start | bytes 884740
  1019.3 241.3 %reduce-scatter.20.cloned.1.call-start = ((), (), s32[]{:S(2)}) async-start(), calls=%async_computation.22 | async-start | bytes 35389440 | tf_op jit(solution)/shard_map/reduce_scatter | solution.py:226
  1059.5 274.8 %reduce-scatter.18.cloned.1.call-start = ((), (), s32[]{:S(2)}) async-start(), calls=%async_computation.21 | async-start | bytes 10321920 | tf_op jit(solution)/shard_map/reduce_scatter | solution.py:141
  1080.6 53.9 %copy-start.22 = (bf16[2688,192]{0,1:T(8,128)(2,1)}, bf16[2688,192]{0,1:T(8,128)(2,1)S(1)}, u32[]{:S(2)}) copy-start(bf16[2688,192]{0,1:T(8,128)(2,1)S(1)} %convert_element_type.281) | copy-start | bytes 3096580
  1139.2 577.7 %all-reduce.5.cloned.1.call-start = ((), (), s32[]{:S(2)}) async-start(), calls=%async_computation.23 | async-start | bytes 18874368 | tf_op jit(solution)/shard_map/psum | solution.py:275
  1274.7 59.6 %copy-start.8 = (bf16[672,768]{1,0:T(8,128)(2,1)S(1)}, bf16[672,768]{1,0:T(8,128)(2,1)}, u32[]{:S(2)}) copy-start(bf16[672,768]{1,0:T(8,128)(2,1)} %param.29) | copy-start | bytes 3096580
  1274.7 59.6 %copy-start.59 = (f32[672]{0:T(1024)S(1)}, f32[672]{0:T(1024)}, u32[]{:S(2)}) copy-start(f32[672]{0:T(1024)} %copy-done.58) | copy-start | bytes 8068
  1274.7 59.6 %copy-start.65 = (f32[768]{0:T(1024)S(1)}, f32[768]{0:T(1024)}, u32[]{:S(2)}) copy-start(f32[768]{0:T(1024)} %copy-done.64) | copy-start | bytes 9220
  1274.7 59.6 %copy-start.67 = (f32[672]{0:T(1024)S(1)}, f32[672]{0:T(1024)}, u32[]{:S(2)}) copy-start(f32[672]{0:T(1024)} %copy-done.66) | copy-start | bytes 8068
  1274.8 62.1 %copy-start.73 = (f32[768]{0:T(1024)S(1)}, f32[768]{0:T(1024)}, u32[]{:S(2)}) copy-start(f32[768]{0:T(1024)} %get-tuple-element.75) | copy-start | bytes 9220
  1274.8 62.1 %copy-start.74 = (f32[768]{0:T(1024)S(1)}, f32[768]{0:T(1024)}, u32[]{:S(2)}) copy-start(f32[768]{0:T(1024)} %get-tuple-element.84) | copy-start | bytes 9220
  1274.8 62.1 %copy-start.75 = (f32[768]{0:T(1024)S(1)}, f32[768]{0:T(1024)}, u32[]{:S(2)}) copy-start(f32[768]{0:T(1024)} %get-tuple-element.27) | copy-start | bytes 9220
  1274.8 62.1 %copy-start.76 = (f32[768]{0:T(1024)S(1)}, f32[768]{0:T(1024)}, u32[]{:S(2)}) copy-start(f32[768]{0:T(1024)} %get-tuple-element.36) | copy-start | bytes 9220
  1274.8 62.1 %copy-start.77 = (f32[768]{0:T(1024)S(1)}, f32[768]{0:T(1024)}, u32[]{:S(2)}) copy-start(f32[768]{0:T(1024)} %get-tuple-element.29) | copy-start | bytes 9220
  1274.8 62.1 %copy-start.78 = (f32[768]{0:T(1024)S(1)}, f32[768]{0:T(1024)}, u32[]{:S(2)}) copy-start(f32[768]{0:T(1024)} %get-tuple-element.37) | copy-start | bytes 9220
  1274.8 62.1 %copy-start.79 = (f32[768]{0:T(1024)S(1)}, f32[768]{0:T(1024)}, u32[]{:S(2)}) copy-start(f32[768]{0:T(1024)} %get-tuple-element.77) | copy-start | bytes 9220
  1274.8 73.4 %copy-start.81 = (f32[768]{0:T(1024)S(1)}, f32[768]{0:T(1024)}, u32[]{:S(2)}) copy-start(f32[768]{0:T(1024)} %get-tuple-element.72) | copy-start | bytes 9220
  1274.8 263.5 %all-to-all-start.1 = ((bf16[6,1536,192]{2,0,1:T(8,128)(2,1)}), bf16[6,1536,192]{2,0,1:T(8,128)(2,1)}, u32[]{:S(2)}, u32[]{:S(2)}) async-start(bf16[6,1536,192]{2,0,1:T(8,128)(2,1)} %copy.121), calls=%async_computation.8 | async-start | bytes 12582912 | tf_op jit(solution)/shard_map/all_to_all | solution.py:227
  1280.4 254.7 %copy-start.14 = (f32[672,768]{1,0:T(8,128)S(1)}, f32[672,768]{1,0:T(8,128)}, u32[]{:S(2)}) copy-start(f32[672,768]{1,0:T(8,128)} %copy-done.13) | copy-start | bytes 6193156
  (68 other events, 356.0 us)
Sparse Core Ops, SparseCore 0:
  15.3 36.8 all-gather.7
  109.8 70.9 reduce-scatter.7
  236.1 89.1 all-gather.9
  327.3 34.1 all-gather.11
  477.0 70.9 reduce-scatter.9
  552.6 34.1 all-gather.13
  588.3 34.1 all-gather.15
  655.5 70.8 reduce-scatter.13
  729.0 70.8 reduce-scatter.11
  806.6 34.0 all-gather.17
  941.3 70.8 reduce-scatter.15
  1019.4 34.0 all-gather.19
  1059.6 200.9 reduce-scatter.19
  1263.3 70.9 reduce-scatter.17
  1343.7 373.0 all-reduce.4
where the time goes:
time: 1750 us; the launch traced here: 1740 us
  waiting for transfers between devices  759 us (43%)
  matrix products  384 us (22%)
  blocking collectives  309 us (18%)
  other arithmetic  156 us (9%)
  local copies, waits for them, and re-layouts  108 us (6%)
    psum x1, blocking collectives, on_device(): lax.psum((grad_query, grad_query_bias, grad_key, grad_value, grad_value_b...  187 us
    psum x1, waiting for transfers between devices, on_device(): lax.psum((grad_query, grad_query_bias, grad_key, grad_value, grad_value_b...  172 us
    reduce_scatter x3, waiting for transfers between devices, input_sum(): lax.psum_scatter(reduce(jnp.add, parts), 'narrow', scatter_dimension=0, t...  149 us
    reduce_scatter x3, waiting for transfers between devices, branch_sum(): lax.psum_scatter(jnp.dot(piece, weight, preferred_element_type=jnp.float3...  140 us
    all_to_all x1, blocking collectives, on_device(): lax.all_to_all(encoded, 'wide', split_axis=0, concat_axis=1, tiled=True)  110 us
    all_gather x1, waiting for transfers between devices, on_device(): source = lax.all_gather(regrouped, 'narrow', axis=2, tiled=True)  82.3 us
    all_gather x3, waiting for transfers between devices, gather_rows(): lax.all_gather(values.astype(jnp.bfloat16), 'narrow', axis=0, tiled=True)  81.5 us
    reduce_scatter x1, waiting for transfers between devices, on_device(): lax.psum_scatter(source_part, 'narrow', scatter_dimension=2, tiled=True)  72.5 us
  transfers between devices with their start and end apart: 16, of which 13 were waited for; matrix products, arithmetic and copies ran while one was open for 16% of the time, Pallas kernels for 0%

commit v1 on v0

v1 whole, which is shorter than its diff:
```python
import functools
import math

import jax
import jax.numpy as jnp
from jax import lax
from jax.experimental import pallas as pl
from jax.experimental.pallas import tpu as pltpu
from jax.sharding import PartitionSpec as P

HDIM=64
NEG=-1e30
SCALE=HDIM**-0.5
LOG2E=math.log2(math.e)
C=SCALE*LOG2E
NT=(((1,),(1,)),((),()))
TN=(((0,),(0,)),((),()))
NN=(((1,),(0,)),((),()))
def _dot(a,b,dims): return lax.dot_general(a,b,dims,preferred_element_type=jnp.float32)

def _masked(s, causal, off, live, base):
    col=lax.broadcasted_iota(jnp.int32,s.shape,1)
    ok=col<live
    if causal:
        row=lax.broadcasted_iota(jnp.int32,s.shape,0)+off
        ok=ok&(col<=row)
    return jnp.where(ok,s,NEG)

def fwd_kernel(off_ref, live_ref, q_ref, kv_ref, o_ref, l_ref, *, causal):
    j=pl.program_id(1)
    off=off_ref[j]; live=live_ref[j]
    bq=q_ref.shape[0]; S=kv_ref.shape[0]
    low=lax.broadcasted_iota(jnp.int32,(bq,128),1)<HDIM
    lowv=lax.broadcasted_iota(jnp.int32,(S,128),1)<HDIM
    one=jnp.ones((S,128),jnp.bfloat16)
    zq=jnp.zeros((bq,128),jnp.bfloat16)
    for g in range(q_ref.shape[1]//128):
        lanes=slice(128*g,128*g+128)
        q=q_ref[:,lanes]
        k=kv_ref[:,256*g:256*g+128]; v=kv_ref[:,256*g+128:256*g+256]
        accs=[];tops=[]
        for h in (0,1):
            mine=low if h==0 else ~low
            minev=lowv if h==0 else ~lowv
            s=_masked(_dot(jnp.where(mine,q,zq),k,NT),causal,off,live,0)
            top=jnp.max(s,axis=1,keepdims=True)
            p=jnp.exp2((s-top)*C).astype(jnp.bfloat16)
            accs.append(_dot(p,jnp.where(minev,v,one),NN))
            tops.append(top)
        total=pltpu.roll(jnp.where(low,accs[1],accs[0]),HDIM,1)
        o_ref[:,lanes]=(jnp.where(low,accs[0],accs[1])/total).astype(o_ref.dtype)
        l_ref[:,lanes]=jnp.where(low,tops[0],tops[1])*C+jnp.log2(total)

def attn_fwd(q, kv, off, live, *, causal, bq, nq, q0, item_of, S, hb=1, vmem=56<<20):
    heads2=q.shape[1]//128//hb
    rows=bq*nq
    return pl.pallas_call(
        functools.partial(fwd_kernel,causal=causal),
        out_shape=(jax.ShapeDtypeStruct((rows,q.shape[1]),jnp.bfloat16),jax.ShapeDtypeStruct((rows,q.shape[1]),jnp.float32)),
        grid_spec=pltpu.PrefetchScalarGridSpec(num_scalar_prefetch=2,grid=(heads2,nq),
            in_specs=[pl.BlockSpec((bq,128*hb),lambda h,j,*_:(q0+j,h)),
                      pl.BlockSpec((S,256*hb),lambda h,j,*_:(item_of(j),h))],
            out_specs=(pl.BlockSpec((bq,128*hb),lambda h,j,*_:(j,h)),pl.BlockSpec((bq,128*hb),lambda h,j,*_:(j,h)))),
        compiler_params=pltpu.CompilerParams(dimension_semantics=("arbitrary","arbitrary"),vmem_limit_bytes=vmem),
        cost_estimate=pl.CostEstimate(flops=hb*heads2*nq*8*bq*S*128,transcendentals=hb*heads2*nq*2*bq*S,bytes_accessed=rows*768*8+S*1536*2),
    )(off,live,q,kv)

def bwd_kernel(off_ref, live_ref, q_ref, kv_ref, do_ref, o_ref, l_ref, dq_ref, dkv_ref, acc_ref, *, causal, first, last, nq):
    j=pl.program_id(1)
    off=off_ref[j]; live=live_ref[j]
    bq=q_ref.shape[0]; S=kv_ref.shape[0]
    low=lax.broadcasted_iota(jnp.int32,(bq,128),1)<HDIM
    lowv=lax.broadcasted_iota(jnp.int32,(S,128),1)<HDIM
    zq=jnp.zeros((bq,128),jnp.bfloat16); zv=jnp.zeros((S,128),jnp.bfloat16)
    is_first=functools.reduce(jnp.logical_or,[j==f for f in first])
    is_last=functools.reduce(jnp.logical_or,[j==f for f in last])
    for g in range(q_ref.shape[1]//128):
        lanes=slice(128*g,128*g+128)
        lk=slice(256*g,256*g+128); lv=slice(256*g+128,256*g+256)
        q=q_ref[:,lanes]; do=do_ref[:,lanes]
        k=kv_ref[:,lk]; v=kv_ref[:,lv]
        prod=do.astype(jnp.float32)*o_ref[:,lanes].astype(jnp.float32)
        stat=l_ref[:,lanes]
        dq=None;dk=None;dv=None
        for h in (0,1):
            mine=low if h==0 else ~low
            minev=lowv if h==0 else ~lowv
            qh=jnp.where(mine,q,zq); doh=jnp.where(mine,do,zq)
            kh=jnp.where(minev,k,zv)
            s=_masked(_dot(qh,k,NT),causal,off,live,0)
            p=jnp.exp2(s*C-stat[:,h*HDIM:h*HDIM+1])
            dp=_dot(doh,v,NT)
            D=jnp.sum(jnp.where(mine,prod,0.0),axis=1,keepdims=True)
            ds=(p*(dp-D)).astype(jnp.bfloat16)
            pb=p.astype(jnp.bfloat16)
            a=_dot(ds,kh,NN); b=_dot(ds,qh,TN); c=_dot(pb,doh,TN)
            dq=a if dq is None else dq+a
            dk=b if dk is None else dk+b
            dv=c if dv is None else dv+c
        dq_ref[:,lanes]=(dq*SCALE).astype(dq_ref.dtype)
        dk=dk*SCALE
        if len(first)==nq:
            dkv_ref[:,lk]=dk.astype(dkv_ref.dtype); dkv_ref[:,lv]=dv.astype(dkv_ref.dtype)
        else:
            @pl.when(is_first)
            def _():
                acc_ref[:,lk]=dk; acc_ref[:,lv]=dv
            @pl.when(jnp.logical_not(is_first))
            def _():
                acc_ref[:,lk]+=dk; acc_ref[:,lv]+=dv
    if len(first)!=nq:
        @pl.when(is_last)
        def _():
            dkv_ref[...]=acc_ref[...].astype(dkv_ref.dtype)

def attn_bwd(q, kv, do, o, stat, off, live, *, causal, bq, nq, q0, do0, s0, item_of, items, first, last, S, hb=1, vmem=60<<20):
    heads2=q.shape[1]//128//hb
    rows=bq*nq
    return pl.pallas_call(
        functools.partial(bwd_kernel,causal=causal,first=first,last=last,nq=nq),
        out_shape=(jax.ShapeDtypeStruct((rows,q.shape[1]),jnp.bfloat16),jax.ShapeDtypeStruct((items*S,2*q.shape[1]),jnp.bfloat16)),
        grid_spec=pltpu.PrefetchScalarGridSpec(num_scalar_prefetch=2,grid=(heads2,nq),
            in_specs=[pl.BlockSpec((bq,128*hb),lambda h,j,*_:(q0+j,h)),
                      pl.BlockSpec((S,256*hb),lambda h,j,*_:(item_of(j),h)),
                      pl.BlockSpec((bq,128*hb),lambda h,j,*_:(do0+j,h)),
                      pl.BlockSpec((bq,128*hb),lambda h,j,*_:(do0+j,h)),
                      pl.BlockSpec((bq,128*hb),lambda h,j,*_:(s0+j,h))],
            out_specs=(pl.BlockSpec((bq,128*hb),lambda h,j,*_:(j,h)),pl.BlockSpec((S,256*hb),lambda h,j,*_:(item_of(j),h))),
            scratch_shapes=[pltpu.VMEM((S if len(first)!=nq else 8,256*hb),jnp.float32)]),
        compiler_params=pltpu.CompilerParams(dimension_semantics=("arbitrary","arbitrary"),vmem_limit_bytes=vmem),
        cost_estimate=pl.CostEstimate(flops=hb*heads2*nq*20*bq*S*128,transcendentals=hb*heads2*nq*2*bq*S,bytes_accessed=rows*768*12+S*1536*4),
    )(off,live,q,kv,do,o,stat)


LEN = 448
HALF = LEN // 2
BF = jnp.bfloat16
F32 = jnp.float32


def mm(a, b, dims):
    return lax.dot_general(a, b, dims, preferred_element_type=F32)


def norm_parts(values):
    center = values - jnp.mean(values, axis=-1, keepdims=True)
    scaled = lax.rsqrt(jnp.mean(center * center, axis=-1, keepdims=True) + 1e-05)
    return center * scaled, scaled


def norm_apply(normal, gain, shift):
    return (normal * gain.astype(F32) + shift.astype(F32)).astype(BF)


def norm_backward(grad, normal, scaled, gain):
    weighted = grad * gain.astype(F32)
    centered = weighted - jnp.mean(weighted, axis=-1, keepdims=True)
    return scaled * (centered - normal * jnp.mean(weighted * normal, axis=-1, keepdims=True))


def interleave(first, second):
    pairs = first.shape[0] // 128
    tail = first.shape[1:]
    return jnp.stack(
        [first.reshape((pairs, 128) + tail), second.reshape((pairs, 128) + tail)], axis=1
    ).reshape((2 * first.shape[0],) + tail)


def separate(both):
    tail = both.shape[1:]
    split = both.reshape((both.shape[0] // 256, 2, 128) + tail)
    flat = (both.shape[0] // 2,) + tail
    return split[:, 0].reshape(flat), split[:, 1].reshape(flat)


def make_body(wide, narrow):
    beside = [(i, i ^ 1) for i in range(narrow)]
    across = [(i, i ^ 2) for i in range(narrow)]

    def on_device(
        tokens,
        encoded,
        lengths,
        enc_frames,
        cotangent,
        attn_gain,
        attn_shift,
        query_weight,
        query_bias,
        key_weight,
        value_weight,
        value_bias,
        output_weight,
        output_bias,
        cross_gain,
        cross_shift,
        lookup_weight,
        lookup_bias,
        source_keys,
        source_values,
        source_bias,
        merged_weight,
        merged_bias,
        dense_gain,
        dense_shift,
        expand_weight,
        expand_bias,
        reduce_weight,
        reduce_bias,
    ):
        rows, width = tokens.shape
        part = width // narrow
        own_frames = encoded.shape[1]
        frames = own_frames * wide
        n = lax.axis_index("narrow")
        odd = lax.rem(n, 2)
        chip = lax.div(n, 2)
        is_odd = odd == 1

        def swap(values):
            return lax.ppermute(values, "narrow", beside)

        def gather(values):
            return lax.all_gather(values, "narrow", axis=0, tiled=True)

        def arrange(values):
            return jnp.where(is_odd, jnp.concatenate([values[HALF:], values[:HALF]]), values)

        def restore(values):
            return jnp.where(is_odd, jnp.concatenate([values[LEN:], values[:LEN]]), values)

        def stacked_gather(parts):
            count = len(parts)
            got = lax.all_gather(jnp.stack(parts), "narrow", axis=0, tiled=False)
            return [got[:, i].reshape(width, width) for i in range(count)]

        query_t, key_t, value_t = stacked_gather([query_weight.T, key_weight.T, value_weight.T])
        output_w, lookup_t, keys_t, values_t, merged_w = stacked_gather(
            [output_weight, lookup_weight.T, source_keys.T, source_values.T, merged_weight]
        )
        expand_t = gather(expand_weight.T)
        reduce_w = gather(reduce_weight)
        biases = lax.all_gather(
            jnp.stack([query_bias, value_bias, lookup_bias, source_bias]), "narrow", axis=1, tiled=True
        ).astype(F32)
        query_b, value_b, lookup_b, source_b = biases[0], biases[1], biases[2], biases[3]
        expand_b = gather(expand_bias).astype(F32)

        mine_in = []
        grouped = encoded.reshape(wide, 2, 3, own_frames, part)
        kept = lax.dynamic_index_in_dim(grouped, chip, 1, keepdims=False)
        sent = lax.dynamic_index_in_dim(grouped, 1 - chip, 1, keepdims=False)
        halfway = own_frames // 2

        def pack(values):
            return jnp.concatenate([values[..., :halfway, :], values[..., halfway:, :]], -1)

        def unpack(values):
            return jnp.concatenate([values[..., :part], values[..., part:]], -2)

        def spread(values):
            return lax.all_to_all(values, "wide", split_axis=0, concat_axis=0, tiled=True)

        def arrive(c):
            got = unpack(lax.ppermute(pack(sent[:, c]), "narrow", across))
            both = jnp.concatenate([kept[:, c], got], -1)
            return spread(both).reshape(frames, 2 * part)

        shared_own = arrive(1)
        first_own = arrive(0)
        last_own = arrive(2)
        shared = jnp.concatenate([shared_own, swap(shared_own)], -1)
        full = jnp.concatenate(
            [
                jnp.where(is_odd, last_own, first_own),
                swap(jnp.where(is_odd, first_own, last_own)),
            ],
            -1,
        )
        order = [n, n ^ 2, n ^ 1, n ^ 3]
        source_t = interleave(keys_t, values_t)
        columns = source_t.reshape(2 * width, narrow, part)
        source_w = jnp.concatenate(
            [lax.dynamic_index_in_dim(columns, o, 1, keepdims=False) for o in order], -1
        )
        source_bb = interleave(jnp.zeros_like(source_b), source_b)

        item_full = 3 * chip + 2 * odd
        item_half = 3 * chip + 1
        len_full, len_half = lengths[item_full], lengths[item_half]
        live_full, live_half = enc_frames[item_full], enc_frames[item_half]
        zero = jnp.int32(0)

        rows_in = arrange(tokens)
        half_own = rows_in[LEN:]
        half_got = swap(half_own)
        extended = jnp.concatenate(
            [
                rows_in[:LEN],
                jnp.where(is_odd, half_got, half_own),
                jnp.where(is_odd, half_own, half_got),
            ]
        ).astype(F32)
        normal_ext, unused = norm_parts(extended)
        first_ext = norm_apply(normal_ext, attn_gain, attn_shift)
        rows_in = rows_in.astype(F32)
        normal_self, scaled_self = norm_parts(rows_in)
        first = norm_apply(normal_self, attn_gain, attn_shift)
        pair_t = interleave(key_t, value_t)
        pair_b = interleave(jnp.zeros_like(value_b), value_b)
        query = (mm(first, query_t, NT) + query_b).astype(BF)
        pair = (mm(first_ext, pair_t, NT) + pair_b).astype(BF)
        self_off = jnp.stack([zero, jnp.int32(HALF), odd * HALF])
        self_live = jnp.stack([len_full, len_full, len_half])
        attended, stat_self = attn_fwd(
            query, pair, self_off, self_live,
            causal=True, bq=HALF, nq=3, q0=0, item_of=lambda j: j // 2, S=LEN, hb=3,
        )
        after_self = rows_in + mm(attended, output_w, NN) + output_bias.astype(F32)

        normal_cross, scaled_cross = norm_parts(after_self)
        second = norm_apply(normal_cross, cross_gain, cross_shift)
        lookup = (mm(second, lookup_t, NT) + lookup_b).astype(BF)
        heard_half = (mm(shared, source_w, NT) + source_bb).astype(BF)
        heard_full = (mm(full, source_w, NT) + source_bb).astype(BF)
        none = jnp.zeros((1,), jnp.int32)
        one_item = dict(causal=False, nq=1, item_of=lambda j: 0, S=frames)
        recalled_half, stat_half = attn_fwd(
            lookup, heard_half, none, live_half.reshape(1), bq=HALF, q0=2, hb=2, **one_item
        )
        recalled_full, stat_full = attn_fwd(
            lookup, heard_full, none, live_full.reshape(1), bq=LEN, q0=0, hb=3, **one_item
        )
        recalled = jnp.concatenate([recalled_full, recalled_half])
        after_cross = after_self + mm(recalled, merged_w, NN) + merged_bias.astype(F32)

        normal_dense, scaled_dense = norm_parts(after_cross)
        third = norm_apply(normal_dense, dense_gain, dense_shift)
        widened = mm(third, expand_t, NT) + expand_b
        below = 0.5 * (1.0 + lax.erf(widened * math.sqrt(0.5)))
        activated = (widened * below).astype(BF)
        slope = (
            below + widened * (jnp.exp(-0.5 * widened * widened) * (1.0 / math.sqrt(2.0 * math.pi)))
        ).astype(BF)
        result = (
            after_cross + mm(activated, reduce_w, NN) + reduce_bias.astype(F32)
        ).astype(BF)
        spread_dense = arrange(cotangent)
        grad_out = spread_dense.astype(F32)
        grad_reduce_bias = jnp.sum(grad_out, axis=0)
        grad_widened = (mm(spread_dense, reduce_w, NT) * slope.astype(F32)).astype(BF)
        grad_reduce = mm(activated, spread_dense, TN)
        grad_expand = mm(grad_widened, third, TN)
        grad_expand_bias = jnp.sum(grad_widened.astype(F32), axis=0)
        back_dense = mm(grad_widened, expand_t, NN)
        grad_dense_gain = jnp.sum(back_dense * normal_dense, axis=0)
        grad_dense_shift = jnp.sum(back_dense, axis=0)
        grad_after_cross = grad_out + norm_backward(
            back_dense, normal_dense, scaled_dense, dense_gain
        )

        def over_wide(values):
            share = values.shape[0] // wide
            pieces = lax.all_to_all(values, "wide", split_axis=0, concat_axis=0, tiled=True)
            total = jnp.sum(pieces.reshape(wide, share, width).astype(F32), axis=0)
            return lax.all_gather(total.astype(BF), "wide", axis=0, tiled=True).astype(F32)

        def over_all(values):
            return over_wide(
                lax.psum_scatter(values.astype(BF), "narrow", scatter_dimension=0, tiled=True)
            )

        def over_all_group(parts):
            count = len(parts)
            lined = jnp.stack([p.astype(BF).reshape(narrow, part, width) for p in parts], axis=1)
            summed = over_all(lined.reshape(narrow * count * part, width))
            return [summed[i * part : (i + 1) * part] for i in range(count)]

        sum_reduce = over_all(grad_reduce)
        sum_expand = over_all(grad_expand).T

        grad_merged_bias = jnp.sum(grad_after_cross, axis=0)
        spread_cross = grad_after_cross.astype(BF)
        grad_merged = mm(recalled, spread_cross, TN)
        grad_recalled = mm(spread_cross, merged_w, NT).astype(BF)
        back = dict(causal=False, nq=1, item_of=lambda j: 0, items=1, first=(0,), last=(0,), S=frames, s0=0)
        d_lookup_half, d_heard_half = attn_bwd(
            lookup, heard_half, grad_recalled, recalled, stat_half, none, live_half.reshape(1),
            bq=HALF, q0=2, do0=2, **back,
        )
        d_lookup_full, d_heard_full = attn_bwd(
            lookup, heard_full, grad_recalled, recalled, stat_full, none, live_full.reshape(1),
            bq=LEN, q0=0, do0=0, **back,
        )

        def leave(values):
            moved = spread(values.reshape(wide, own_frames, 2 * part))
            return moved[..., :part], pack(moved[..., part:])

        back_half = mm(d_heard_half, source_w, NN).astype(BF)
        shared_sum = (
            back_half[:, : 2 * part].astype(F32) + swap(back_half[:, 2 * part :]).astype(F32)
        ).astype(BF)
        shared_out = leave(shared_sum)
        back_full = mm(d_heard_full, source_w, NN).astype(BF)
        full_own = back_full[:, : 2 * part]
        full_got = swap(back_full[:, 2 * part :])
        first_out = leave(jnp.where(is_odd, full_got, full_own))
        last_out = leave(jnp.where(is_odd, full_own, full_got))
        outs = [first_out, shared_out, last_out]
        here = jnp.stack([o[0] for o in outs], axis=1)
        there = jnp.stack(
            [unpack(lax.ppermute(o[1], "narrow", across)) for o in outs], axis=1
        )
        low_chip = chip == 0
        encoded_grad = jnp.stack(
            [jnp.where(low_chip, here, there), jnp.where(low_chip, there, here)], axis=1
        ).reshape(encoded.shape)

        d_lookup = jnp.concatenate([d_lookup_full, d_lookup_half])
        grad_lookup_bias = jnp.sum(d_lookup.astype(F32), axis=0)
        grad_lookup = mm(d_lookup, second, TN)
        grad_source = mm(d_heard_full, full, TN) + mm(d_heard_half, shared, TN)
        grad_source = grad_source.astype(BF).reshape(2 * width, narrow, part)
        places = [n, n ^ 1, n ^ 2, n ^ 3]
        table = jnp.array([0, 2, 1, 3], jnp.int32)
        grad_source = jnp.concatenate(
            [
                lax.dynamic_index_in_dim(grad_source, table[n ^ i], 1, keepdims=False)
                for i in range(narrow)
            ],
            -1,
        )
        grad_keys, grad_values = separate(grad_source)
        sum_bias = jnp.sum(d_heard_full.astype(F32), axis=0) + jnp.sum(
            d_heard_half.astype(F32), axis=0
        )
        unused, grad_source_bias = separate(sum_bias)
        back_cross = mm(d_lookup, lookup_t, NN)
        grad_cross_gain = jnp.sum(back_cross * normal_cross, axis=0)
        grad_cross_shift = jnp.sum(back_cross, axis=0)
        grad_after_self = grad_after_cross + norm_backward(
            back_cross, normal_cross, scaled_cross, cross_gain
        )
        sum_lookup, sum_keys, sum_values, sum_merged = over_all_group(
            [grad_lookup, grad_keys, grad_values, grad_merged]
        )

        grad_output_bias = jnp.sum(grad_after_self, axis=0)
        spread_self = grad_after_self.astype(BF)
        grad_output = mm(attended, spread_self, TN)
        grad_attended = mm(spread_self, output_w, NT).astype(BF)
        d_query, d_pair = attn_bwd(
            query, pair, grad_attended, attended, stat_self, self_off, self_live,
            causal=True, bq=HALF, nq=3, q0=0, do0=0, s0=0, item_of=lambda j: j // 2,
            items=2, first=(0, 2), last=(1, 2), S=LEN, hb=3,
        )
        back_ext = mm(d_pair, pair_t, NN)
        near, far = back_ext[LEN : LEN + HALF], back_ext[LEN + HALF :]
        half_back = jnp.where(is_odd, far, near) + swap(jnp.where(is_odd, near, far))
        back_self = jnp.concatenate([back_ext[:LEN], half_back]) + mm(d_query, query_t, NN)
        grad_query_bias = jnp.sum(d_query.astype(F32), axis=0)
        unused, grad_value_bias = separate(jnp.sum(d_pair.astype(F32), axis=0))
        grad_query = mm(d_query, first, TN)
        grad_key, grad_value = separate(mm(d_pair, first_ext, TN))
        sum_query, sum_key, sum_value, sum_output = over_all_group(
            [grad_query, grad_key, grad_value, grad_output]
        )
        grad_attn_gain = jnp.sum(back_self * normal_self, axis=0)
        grad_attn_shift = jnp.sum(back_self, axis=0)
        tokens_grad = (
            grad_after_self + norm_backward(back_self, normal_self, scaled_self, attn_gain)
        ).astype(BF)

        small = lax.psum(
            jnp.concatenate(
                [
                    jnp.stack(
                        [
                            grad_attn_gain,
                            grad_attn_shift,
                            grad_output_bias,
                            grad_cross_gain,
                            grad_cross_shift,
                            grad_merged_bias,
                            grad_dense_gain,
                            grad_dense_shift,
                            grad_reduce_bias,
                            grad_query_bias,
                            grad_value_bias,
                            grad_lookup_bias,
                            grad_source_bias,
                        ]
                    ),
                    grad_expand_bias.reshape(-1, width),
                ]
            ),
            ("wide", "narrow"),
        )

        def own(vector):
            share = vector.shape[0] // narrow
            return lax.dynamic_slice_in_dim(vector, n * share, share)

        return (
            restore(result),
            restore(tokens_grad),
            encoded_grad,
            small[0],
            small[1],
            sum_query.T,
            own(small[9]),
            sum_key.T,
            sum_value.T,
            own(small[10]),
            sum_output,
            small[2],
            small[3],
            small[4],
            sum_lookup.T,
            own(small[11]),
            sum_keys.T,
            sum_values.T,
            own(small[12]),
            sum_merged,
            small[5],
            small[6],
            small[7],
            sum_expand,
            own(small[13:].reshape(-1)),
            sum_reduce,
            small[8],
        )

    return on_device


def solution(mesh):
    placed = (
        P(("wide", "narrow"), None),
        P(None, "wide", "narrow"),
        P("wide"),
        P("wide"),
        P(("wide", "narrow"), None),
        P(),
        P(),
        P(None, "narrow"),
        P("narrow"),
        P(None, "narrow"),
        P(None, "narrow"),
        P("narrow"),
        P("narrow", None),
        P(),
        P(),
        P(),
        P(None, "narrow"),
        P("narrow"),
        P(None, "narrow"),
        P(None, "narrow"),
        P("narrow"),
        P("narrow", None),
        P(),
        P(),
        P(),
        P(None, "narrow"),
        P("narrow"),
        P("narrow", None),
        P(),
    )
    return jax.shard_map(
        make_body(mesh.shape["wide"], mesh.shape["narrow"]),
        mesh=mesh,
        in_specs=placed,
        out_specs=(
            P(("wide", "narrow"), None),
            P(("wide", "narrow"), None),
            P(None, "wide", "narrow"),
            P(),
            P(),
            P(None, "narrow"),
            P("narrow"),
            P(None, "narrow"),
            P(None, "narrow"),
            P("narrow"),
            P("narrow", None),
            P(),
            P(),
            P(),
            P(None, "narrow"),
            P("narrow"),
            P(None, "narrow"),
            P(None, "narrow"),
            P("narrow"),
            P("narrow", None),
            P(),
            P(),
            P(),
            P(None, "narrow"),
            P("narrow"),
            P("narrow", None),
            P(),
        ),
        check_vma=False,
    )
```

time: 1750 us -> 812 us (0.46)
  waiting for transfers between devices: 759 us -> 204 us
  matrix products: 384 us -> 130 us
  blocking collectives: 309 us -> 109 us
  Pallas kernels: 0 us -> 118 us
  other arithmetic: 156 us -> 66.9 us
  starting transfers between devices: 6.98 us -> 55.3 us
    reduce_scatter x7 -> x4, waiting for transfers between devices: 362 us -> 0.06 us  [over_all(): lax.psum_scatter(values.astype(BF), 'narrow', scatter_dimension=0, tiled=...]
    dot_general x41 -> x27, matrix products: 369 us -> 130 us  [mm(): return lax.dot_general(a, b, dims, preferred_element_type=F32)]
    all_gather x7 -> x8, waiting for transfers between devices: 224 us -> 27.3 us  [the longest x4 27.3 us: over_wide(): lax.all_gather(total.astype(BF), 'wide', axis=0, tiled=True).astype(F32)]
    psum x1 -> x0, waiting for transfers between devices: 172 us -> none  [on_device(): lax.psum((grad_query, grad_query_bias, grad_key, grad_value, grad_value_b...]
    psum x2 -> x1, blocking collectives: 198 us -> 49.3 us  [on_device(): lax.psum(jnp.concatenate([jnp.stack([grad_attn_gain, grad_attn_shift, gra...]
    all_to_all x1 -> x9, waiting for transfers between devices: 0.01 us -> 118 us  [the longest x4 67.1 us: over_wide(): lax.all_to_all(values, 'wide', split_axis=0, concat_axis=0, tiled=True)]
    pallas_call x0 -> x6, Pallas kernels: none -> 118 us  [the longest x3 75.1 us: attn_bwd(): pl.pallas_call(functools.partial(bwd_kernel, causal=causal, first=first,...]
    all_to_all x1, blocking collectives: 110 us -> 32.6 us  [spread(): lax.all_to_all(values, 'wide', split_axis=0, concat_axis=0, tiled=True)]
  transfers between devices with their start and end apart: 16 -> 33, of which waited for: 13 -> 14; matrix products, arithmetic and copies ran while one was open for 16% -> 32% of each run, Pallas kernels for 0% -> 15%
where the time goes in v1:
time: 812 us; the launch traced here: 801 us
  waiting for transfers between devices  204 us (25%)
  matrix products  130 us (16%)
  Pallas kernels  118 us (15%)
  blocking collectives  109 us (13%)
  local copies, waits for them, and re-layouts  93.4 us (12%)
  other arithmetic  66.9 us (8%)
  starting transfers between devices  55.3 us (7%)
  between operations  24.3 us (3%)
    dot_general x27, matrix products, mm(): return lax.dot_general(a, b, dims, preferred_element_type=F32)  130 us
    pallas_call x3, Pallas kernels, attn_bwd(): pl.pallas_call(functools.partial(bwd_kernel, causal=causal, first=first,...  75.1 us
    all_to_all x4, waiting for transfers between devices, over_wide(): lax.all_to_all(values, 'wide', split_axis=0, concat_axis=0, tiled=True)  67.1 us
    all_to_all x5, waiting for transfers between devices, spread(): lax.all_to_all(values, 'wide', split_axis=0, concat_axis=0, tiled=True)  50.8 us
    psum x1, blocking collectives, on_device(): lax.psum(jnp.concatenate([jnp.stack([grad_attn_gain, grad_attn_shift, gra...  49.3 us
    pallas_call x3, Pallas kernels, attn_fwd(): pl.pallas_call(functools.partial(fwd_kernel, causal=causal), out_shape=(j...  42.4 us
    ppermute x3, waiting for transfers between devices, arrive(): got = unpack(lax.ppermute(pack(sent[:, c]), 'narrow', across))  33.6 us
    all_to_all x1, blocking collectives, spread(): lax.all_to_all(values, 'wide', split_axis=0, concat_axis=0, tiled=True)  32.6 us
  transfers between devices with their start and end apart: 33, of which 14 were waited for; matrix products, arithmetic and copies ran while one was open for 32% of the time, Pallas kernels for 15%

profile of v1, /device:TPU:0, one launch (start us, length us, event | category | flops | bytes accessed | tf_op | source)
XLA Modules:
  0.0 800.6 jit_solution(5028830927799651185)
XLA Ops:
  19.7 22.8 %collective-permute-done.4 = bf16[8,96,384]{2,1,0:T(8,128)(2,1)S(1)} collective-permute-done((bf16[8,96,384]{2,1,0:T(8,128)(2,1)S(1)}, bf16[8,96,384]{2,1,0:T(8,128)(2,1)S(1)}, u32[]{:S(2)}, u32[]{:S(2)}) %collective-permute-start.4) | collective-permute-done | bytes 589856 | tf_op jit(solution)/shard_map/ppermute | solution.py:265
  44.2 5.9 all-to-all-start.2
  52.8 10.7 %collective-permute-done.1 = bf16[8,96,384]{2,1,0:T(8,128)(2,1)S(1)} collective-permute-done((bf16[8,96,384]{2,1,0:T(8,128)(2,1)S(1)}, bf16[8,96,384]{2,1,0:T(8,128)(2,1)S(1)}, u32[]{:S(2)}, u32[]{:S(2)}) %collective-permute-start.1) | collective-permute-done | bytes 589856 | tf_op jit(solution)/shard_map/ppermute | solution.py:265
  65.2 10.6 %all-to-all-done.2 = bf16[8,192,384]{2,1,0:T(8,128)(2,1)} async-done(((bf16[8,192,384]{2,1,0:T(8,128)(2,1)}), bf16[8,192,384]{2,1,0:T(8,128)(2,1)}, u32[]{:S(2)}, u32[]{:S(2)}) %all-to-all-start.2) | async-done | bytes 1179680 | tf_op jit(solution)/shard_map/all_to_all | solution.py:262
  88.2 22.2 %all-gather.2 = bf16[4,192,4]{1,2,0:T(4,128)(2,1)S(1)} all-gather(bf16[1,192,4]{1,2,0:T(4,128)(2,1)S(1)} %maximum_bitcast_fusion.3), channel_id=1, replica_groups=mesh['wide'=8,'narrow'=4] {'narrow'}, dimensions={0}, use_global_device_ids=true | all-gather | bytes 7680 | tf_op jit(solution)/shard_map/all_gather | solution.py:243
  110.7 5.3 all-gather.3
  120.1 5.9 all-to-all-start.1
  134.2 21.1 %all-to-all-done.1 = bf16[8,192,384]{2,1,0:T(8,128)(2,1)} async-done(((bf16[8,192,384]{2,1,0:T(8,128)(2,1)}), bf16[8,192,384]{2,1,0:T(8,128)(2,1)}, u32[]{:S(2)}, u32[]{:S(2)}) %all-to-all-start.1) | async-done | bytes 1179680 | tf_op jit(solution)/shard_map/all_to_all | solution.py:262
  161.8 5.4 add_convert_fusion.2.kv_ref
  169.3 15.0 %shard_map.493 = (bf16[672,768]{1,0:T(8,128)(2,1)}, f32[672,768]{1,0:T(8,128)}) custom-call(s32[3]{0:T(128)} %get-tuple-element.200.off_ref, s32[3]{0:T(128)} %get-tuple-element.201.live_ref, bf16[672,768]{1,0:T(8,128)(2,1)} %add_convert_fusion.9.q_ref, bf16[896,1536]{1,0:T(8,128)(2,1)} %add_convert_fusion.2.kv_ref), custom_call_target="tpu_custom_call" | custom-call | flops 1849688064 | bytes 5505024 | tf_op jit(solution)/shard_map/pallas_call | solution.py:57
  184.4 4.6 fusion.43
  191.6 4.4 copy.115
  196.0 5.3 reshape_reshape.3
  203.0 6.9 add_convert_fusion.1.kv_ref
  213.3 16.3 %shard_map.494 = (bf16[448,768]{1,0:T(8,128)(2,1)}, f32[448,768]{1,0:T(8,128)}) custom-call(s32[1]{0:T(128)} %constant.83.clone.1.off_ref, s32[1]{0:T(128)} %get-tuple-element.187.live_ref, bf16[672,768]{1,0:T(8,128)(2,1)} %add_convert_fusion.7.q_ref, bf16[1536,1536]{1,0:T(8,128)(2,1)} %add_convert_fusion.1.kv_ref), custom_call_target="tpu_custom_call" | custom-call | flops 4227858432 | bytes 7471104 | tf_op jit(solution)/shard_map/pallas_call | solution.py:57
  230.8 7.2 add_convert_fusion.kv_ref
  238.0 11.0 %shard_map.495 = (bf16[224,768]{1,0:T(8,128)(2,1)}, f32[224,768]{1,0:T(8,128)}) custom-call(s32[1]{0:T(128)} %constant.83.clone.1.off_ref, s32[1]{0:T(128)} %get-tuple-element.186.live_ref, bf16[672,768]{1,0:T(8,128)(2,1)} %add_convert_fusion.7.q_ref, bf16[1536,1536]{1,0:T(8,128)(2,1)} %add_convert_fusion.kv_ref), custom_call_target="tpu_custom_call" | custom-call | flops 2113929216 | bytes 6094848 | tf_op jit(solution)/shard_map/pallas_call | solution.py:57
  253.8 9.9 %multiply_convert_fusion.1 = (bf16[672,3072]{1,0:T(8,128)(2,1)}, f32[672,3072]{1,0:T(8,128)}) fusion(f32[3072]{0:T(1024)S(1)} %bitcast.243, bf16[3072,768]{0,1:T(8,128)(2,1)} %all-gather.13.cloned.1.call-done, f32[672,768]{1,0:T(8,128)S(1)} %get-tuple-element.193, f32[768]{0:T(1024)S(1)} %convert_element_type.216, f32[768]{0:T(1024)S(1)} %convert_element_type.215, ...), kind=kOutput, calls=%fused_computation.12 | convolution fusion | flops 3185860608 | bytes 19193088 | tf_op jit(solution)/shard_map/dot_general | solution.py:142
  263.7 9.0 %convert_reduce_fusion.2 = (f32[3072]{0:T(1024)S(1)}, bf16[672,3072]{1,0:T(8,128)(2,1)S(1)}) fusion(f32[672,3072]{1,0:T(8,128)} %get-tuple-element.195, f32[3072]{0:T(1024)S(1)} %bitcast.244, bf16[672,768]{1,0:T(8,128)(2,1)} %get-tuple-element.104, bf16[3072,768]{1,0:T(8,128)(2,1)} %all-gather.15.cloned.1.call-done), kind=kOutput, calls=%fused_computation.10 | convolution fusion | flops 3201856512 | bytes 18161664 | tf_op jit(solution)/shard_map/dot_general | solution.py:142
  274.7 6.1 convolution_convert_fusion.1
  289.8 7.9 multiply_reduce_fusion
  301.0 18.0 %shard_map.497 = (bf16[224,768]{1,0:T(8,128)(2,1)}, bf16[1536,1536]{1,0:T(8,128)(2,1)}) custom-call(s32[1]{0:T(128)} %constant.83.clone.1.off_ref, s32[1]{0:T(128)} %get-tuple-element.186.live_ref, bf16[672,768]{1,0:T(8,128)(2,1)} %add_convert_fusion.7.q_ref, bf16[1536,1536]{1,0:T(8,128)(2,1)} %add_convert_fusion.kv_ref, ...), custom_call_target="tpu_custom_call" | custom-call | flops 5284823040 | bytes 11501568 | tf_op jit(solution)/shard_map/pallas_call | solution.py:119
  319.0 9.2 %fusion.27 = f32[1536,768]{0,1:T(8,128)} fusion(bf16[1536,1536]{1,0:T(8,128)(2,1)} %get-tuple-element.50, bf16[1536,384]{1,0:T(8,128)(2,1)} %collective-permute-done.5, bf16[1536,384]{1,0:T(8,128)(2,1)} %bitcast.43), kind=kOutput, calls=%fused_computation.92 | convolution fusion | flops 3628597248 | bytes 11796480 | tf_op jit(solution)/shard_map/dot_general | solution.py:142
  328.1 31.8 %shard_map.496 = (bf16[448,768]{1,0:T(8,128)(2,1)}, bf16[1536,1536]{1,0:T(8,128)(2,1)}) custom-call(s32[1]{0:T(128)} %constant.83.clone.1.off_ref, s32[1]{0:T(128)} %get-tuple-element.187.live_ref, bf16[672,768]{1,0:T(8,128)(2,1)} %add_convert_fusion.7.q_ref, bf16[1536,1536]{1,0:T(8,128)(2,1)} %add_convert_fusion.1.kv_ref, ...), custom_call_target="tpu_custom_call" | custom-call | flops 10569646080 | bytes 13565952 | tf_op jit(solution)/shard_map/pallas_call | solution.py:119
  360.0 8.0 add_convert_fusion.3
  373.1 4.7 fusion.45
  377.8 6.4 copy.121
  384.1 4.4 copy.122
  404.9 25.3 %shard_map.498 = (bf16[672,768]{1,0:T(8,128)(2,1)}, bf16[896,1536]{1,0:T(8,128)(2,1)}) custom-call(s32[3]{0:T(128)} %get-tuple-element.200.off_ref, s32[3]{0:T(128)} %get-tuple-element.201.live_ref, bf16[672,768]{1,0:T(8,128)(2,1)} %add_convert_fusion.9.q_ref, bf16[896,1536]{1,0:T(8,128)(2,1)} %add_convert_fusion.2.kv_ref, ...), custom_call_target="tpu_custom_call" | custom-call | flops 4624220160 | bytes 8945664 | tf_op jit(solution)/shard_map/pallas_call | solution.py:119
  430.2 4.8 convolution_convert_fusion.2
  441.4 7.0 convolution_convert_fusion.4
  450.3 5.8 convolution_convert_fusion
  463.3 6.5 convolution_convert_fusion.3
  473.3 19.1 %all-to-all-done.3 = bf16[8,192,384]{2,1,0:T(8,128)(2,1)S(1)} async-done(((bf16[8,192,384]{2,1,0:T(8,128)(2,1)}), bf16[8,192,384]{2,1,0:T(8,128)(2,1)S(1)}, u32[]{:S(2)}, u32[]{:S(2)}) %all-to-all-start.3) | async-done | bytes 1179680 | tf_op jit(solution)/shard_map/all_to_all | solution.py:262
  492.4 32.6 %all_to_all.66 = bf16[8,192,384]{2,1,0:T(8,128)(2,1)} all-to-all(bf16[8,192,384]{2,1,0:T(8,128)(2,1)S(1)} %bitcast.208), channel_id=1, replica_groups=mesh['wide'=8,'narrow'=4] {'wide'}, dimensions={0} | all-to-all | bytes 2359296 | tf_op jit(solution)/shard_map/all_to_all | solution.py:262
  525.0 4.4 all-to-all-start.8
  529.5 27.7 %all-to-all-done.8 = bf16[8,96,768]{2,1,0:T(8,128)(2,1)} async-done(((bf16[8,96,768]{2,1,0:T(8,128)(2,1)}), bf16[8,96,768]{2,1,0:T(8,128)(2,1)}, u32[]{:S(2)}, u32[]{:S(2)}) %all-to-all-start.8) | async-done | bytes 1179680 | tf_op jit(solution)/shard_map/all_to_all | solution.py:364
  557.2 4.3 all-to-all-start.7
  561.6 7.0 add_convert_fusion.5
  579.4 10.2 %all-to-all-done.7 = bf16[8,96,768]{2,1,0:T(8,128)(2,1)} async-done(((bf16[8,96,768]{2,1,0:T(8,128)(2,1)}), bf16[8,96,768]{2,1,0:T(8,128)(2,1)}, u32[]{:S(2)}, u32[]{:S(2)}) %all-to-all-start.7) | async-done | bytes 1179680 | tf_op jit(solution)/shard_map/all_to_all | solution.py:364
  589.6 4.2 all-to-all-start.6
  611.8 22.4 %all-to-all-done.6 = bf16[8,96,768]{2,1,0:T(8,128)(2,1)} async-done(((bf16[8,96,768]{2,1,0:T(8,128)(2,1)}), bf16[8,96,768]{2,1,0:T(8,128)(2,1)}, u32[]{:S(2)}, u32[]{:S(2)}) %all-to-all-start.6) | async-done | bytes 1179680 | tf_op jit(solution)/shard_map/all_to_all | solution.py:364
  642.8 49.3 %psum.7 = f32[17,768]{1,0:T(8,128)S(1)} all-reduce(f32[17,768]{1,0:T(8,128)S(1)} %concatenate.147), channel_id=1, replica_groups=mesh['wide'=8,'narrow'=4] {'wide','narrow'}, use_global_device_ids=true, to_apply=%region_29.30 | all-reduce | flops 13056 | bytes 104448 | tf_op jit(solution)/shard_map/psum | solution.py:475
  700.6 5.7 all-to-all-start.9
  716.8 7.5 collective-permute-done.9
  724.5 12.5 %collective-permute-done.10 = bf16[8,96,384]{2,1,0:T(8,128)(2,1)S(1)} collective-permute-done((bf16[8,96,384]{2,1,0:T(8,128)(2,1)S(1)}, bf16[8,96,384]{2,1,0:T(8,128)(2,1)S(1)}, u32[]{:S(2)}, u32[]{:S(2)}) %collective-permute-start.10) | collective-permute-done | bytes 589856 | tf_op jit(solution)/shard_map/ppermute | solution.py:413
  737.1 6.7 all-to-all-done.9
  763.3 27.3 %all-gather.23.cloned.1.call-done = bf16[768,768]{1,0:T(8,128)(2,1)} async-done(((bf16[96,768]{1,0:T(8,128)(2,1)}), bf16[768,768]{1,0:T(8,128)(2,1)}) %all-gather.23.cloned.1.call-update) | async-done | bytes 1179664 | tf_op jit(solution)/shard_map/all_gather | solution.py:366
  (430 shorter events, 189.8 us)
Async XLA Ops:
  7.2 150.9 %all-gather.25.cloned.1.call-start = ((), (), s32[]{:S(2)}) async-start(), calls=%async_computation.24 | async-start | bytes 4423680 | tf_op jit(solution)/shard_map/all_gather | solution.py:234
  9.5 174.8 %all-gather.27.cloned.1.call-start = ((), (), s32[]{:S(2)}) async-start(), calls=%async_computation.25 | async-start | bytes 7372800 | tf_op jit(solution)/shard_map/all_gather | solution.py:234
  11.6 242.1 %all-gather.13.cloned.1.call-start = ((), (), s32[]{:S(2)}) async-start(), calls=%async_computation.14 | async-start | bytes 5898240 | tf_op jit(solution)/shard_map/all_gather | solution.py:224
  15.6 26.9 %collective-permute-start.4 = (bf16[8,96,384]{2,1,0:T(8,128)(2,1)S(1)}, bf16[8,96,384]{2,1,0:T(8,128)(2,1)S(1)}, u32[]{:S(2)}, u32[]{:S(2)}) collective-permute-start(bf16[8,96,384]{2,1,0:T(8,128)(2,1)S(1)} %pad_maximum_fusion.18), channel_id=1, source_target_pairs={{0,2},{1,3},{2,0},{3,1},{4,6},{5,7},{6,4},{7,5},{8,10},{9,11},{10,... | collective-permute-start | bytes 1769480 | tf_op jit(solution)/shard_map/ppermute | solution.py:265
  44.2 31.6 %all-to-all-start.2 = ((bf16[8,192,384]{2,1,0:T(8,128)(2,1)}), bf16[8,192,384]{2,1,0:T(8,128)(2,1)}, u32[]{:S(2)}, u32[]{:S(2)}) async-start(bf16[8,192,384]{2,1,0:T(8,128)(2,1)} %maximum_maximum_fusion.2), calls=%async_computation.2 | async-start | bytes 2359296 | tf_op jit(solution)/shard_map/all_to_all | solution.py:262
  50.3 13.3 %collective-permute-start.1 = (bf16[8,96,384]{2,1,0:T(8,128)(2,1)S(1)}, bf16[8,96,384]{2,1,0:T(8,128)(2,1)S(1)}, u32[]{:S(2)}, u32[]{:S(2)}) collective-permute-start(bf16[8,96,384]{2,1,0:T(8,128)(2,1)S(1)} %pad_maximum_fusion.16), channel_id=1, source_target_pairs={{0,2},{1,3},{2,0},{3,1},{4,6},{5,7},{6,4},{7,5},{8,10},{9,11},{10,... | collective-permute-start | bytes 1769480 | tf_op jit(solution)/shard_map/ppermute | solution.py:265
  75.8 44.3 %all-to-all-start = ((bf16[8,192,384]{2,1,0:T(8,128)(2,1)}), bf16[8,192,384]{2,1,0:T(8,128)(2,1)S(1)}, u32[]{:S(2)}, u32[]{:S(2)}) async-start(bf16[8,192,384]{2,1,0:T(8,128)(2,1)} %maximum_maximum_fusion), calls=%async_computation | async-start | bytes 2359296 | tf_op jit(solution)/shard_map/all_to_all | solution.py:262
  79.4 184.3 %all-gather.15.cloned.1.call-start = ((), (), s32[]{:S(2)}) async-start(), calls=%async_computation.15 | async-start | bytes 5898240 | tf_op jit(solution)/shard_map/all_gather | solution.py:224
  80.6 36.8 %collective-permute-start.2 = (bf16[8,96,384]{2,1,0:T(8,128)(2,1)}, bf16[8,96,384]{2,1,0:T(8,128)(2,1)}, u32[]{:S(2)}, u32[]{:S(2)}) collective-permute-start(bf16[8,96,384]{2,1,0:T(8,128)(2,1)} %pad_maximum_fusion.17), channel_id=1, source_target_pairs={{0,2},{1,3},{2,0},{3,1},{4,6},{5,7},{6,4},{7,5},{8,10},{9,11},{10,... | collective-permute-start | bytes 1769480 | tf_op jit(solution)/shard_map/ppermute | solution.py:265
  85.5 46.3 %collective-permute-start = (bf16[224,768]{1,0:T(8,128)(2,1)}, bf16[224,768]{1,0:T(8,128)(2,1)}, u32[]{:S(2)}, u32[]{:S(2)}) collective-permute-start(bf16[224,768]{1,0:T(8,128)(2,1)} %slice.374), channel_id=1, source_target_pairs={{0,1},{1,0},{2,3},{3,2},{4,5},{5,4},{6,7},{7,6},{8,9},{9,8},{10,11... | collective-permute-start | bytes 1032200 | tf_op jit(solution)/shard_map/ppermute | solution.py:221
  85.7 30.4 %copy-start.74 = (bf16[768]{0:T(1024)(128)(2,1)S(1)}, bf16[768]{0:T(1024)(128)(2,1)}, u32[]{:S(2)}) copy-start(bf16[768]{0:T(1024)(128)(2,1)} %param.54) | copy-start | bytes 4612
  85.7 30.4 %copy-start.76 = (s32[6]{0:T(128)S(1)}, s32[6]{0:T(128)}, u32[]{:S(2)}) copy-start(s32[6]{0:T(128)} %param.32) | copy-start | bytes 76
  85.7 31.0 %copy-start.77 = (s32[6]{0:T(128)S(1)}, s32[6]{0:T(128)}, u32[]{:S(2)}) copy-start(s32[6]{0:T(128)} %param.33) | copy-start | bytes 76
  85.8 75.0 %copy-start.15 = (bf16[448,768]{1,0:T(8,128)(2,1)}, bf16[448,768]{1,0:T(8,128)(2,1)S(1)}, u32[]{:S(2)}) copy-start(bf16[448,768]{1,0:T(8,128)(2,1)S(1)} %slice.373) | copy-start | bytes 2064388
  120.1 35.1 %all-to-all-start.1 = ((bf16[8,192,384]{2,1,0:T(8,128)(2,1)}), bf16[8,192,384]{2,1,0:T(8,128)(2,1)}, u32[]{:S(2)}, u32[]{:S(2)}) async-start(bf16[8,192,384]{2,1,0:T(8,128)(2,1)} %maximum_maximum_fusion.1), calls=%async_computation.1 | async-start | bytes 2359296 | tf_op jit(solution)/shard_map/all_to_all | solution.py:262
  126.1 398.9 %reduce-scatter.9.cloned.1.call-start = ((), (), s32[]{:S(2)}) async-start(), calls=%async_computation.20 | async-start | bytes 5898240 | tf_op jit(solution)/shard_map/reduce_scatter | solution.py:370
  126.1 41.0 %copy-start.61 = (f32[672]{0:T(1024)}, f32[672]{0:T(1024)S(1)}, u32[]{:S(2)}) copy-start(f32[672]{0:T(1024)S(1)} %broadcast_multiply_fusion.9) | copy-start | bytes 8068
  126.6 40.5 %copy-start.64 = (f32[672]{0:T(1024)}, f32[672]{0:T(1024)S(1)}, u32[]{:S(2)}) copy-start(f32[672]{0:T(1024)S(1)} %add_rsqrt_fusion.3) | copy-start | bytes 8068
  134.1 96.6 %collective-permute-start.5 = (bf16[1536,384]{1,0:T(8,128)(2,1)}, bf16[1536,384]{1,0:T(8,128)(2,1)}, u32[]{:S(2)}, u32[]{:S(2)}) collective-permute-start(bf16[1536,384]{1,0:T(8,128)(2,1)} %bitcast.43), channel_id=1, source_target_pairs={{0,1},{1,0},{2,3},{3,2},{4,5},{5,4},{6,7},{7,6},{8,9},{9,8},{10,11... | collective-permute-start | bytes 3538952 | tf_op jit(solution)/shard_map/ppermute | solution.py:221
  158.1 43.5 %collective-permute-start.3 = (bf16[1536,384]{1,0:T(8,128)(2,1)}, bf16[1536,384]{1,0:T(8,128)(2,1)}, u32[]{:S(2)}, u32[]{:S(2)}) collective-permute-start(bf16[1536,384]{1,0:T(8,128)(2,1)} %bitcast.34), channel_id=1, source_target_pairs={{0,1},{1,0},{2,3},{3,2},{4,5},{5,4},{6,7},{7,6},{8,9},{9,8},{10,11... | collective-permute-start | bytes 3538952 | tf_op jit(solution)/shard_map/ppermute | solution.py:221
  201.6 29.2 %copy-start.47 = (bf16[1536,192]{0,1:T(8,128)(2,1)}, bf16[1536,192]{0,1:T(8,128)(2,1)S(1)}, u32[]{:S(2)}) copy-start(bf16[1536,192]{0,1:T(8,128)(2,1)S(1)} %get-tuple-element.146) | copy-start | bytes 1769476
  253.3 44.4 %copy-start.8 = (f32[672,768]{1,0:T(8,128)}, f32[672,768]{1,0:T(8,128)S(1)}, u32[]{:S(2)}) copy-start(f32[672,768]{1,0:T(8,128)S(1)} %get-tuple-element.193) | copy-start | bytes 6193156
  280.8 248.7 %reduce-scatter.7.cloned.1.call-start = ((), (), s32[]{:S(2)}) async-start(), calls=%async_computation.18 | async-start | bytes 5898240 | tf_op jit(solution)/shard_map/reduce_scatter | solution.py:370
  328.1 31.8 %copy-start.44 = (bf16[8,192,384]{2,1,0:T(8,128)(2,1)S(1)}, bf16[8,192,384]{2,1,0:T(8,128)(2,1)}, u32[]{:S(2)}) copy-start(bf16[8,192,384]{2,1,0:T(8,128)(2,1)} %get-tuple-element.150) | copy-start | bytes 3538948
  398.4 181.0 %reduce-scatter.5.cloned.1.call-start = ((), (), s32[]{:S(2)}) async-start(), calls=%async_computation.16 | async-start | bytes 5898240 | tf_op jit(solution)/shard_map/reduce_scatter | solution.py:370
  402.4 32.8 %copy-start = (f32[672,768]{1,0:T(8,128)}, f32[672,768]{1,0:T(8,128)S(1)}, u32[]{:S(2)}) copy-start(f32[672,768]{1,0:T(8,128)S(1)} %get-tuple-element.108) | copy-start | bytes 6193156
  441.3 259.3 %reduce-scatter.11.cloned.1.call-start = ((), (), s32[]{:S(2)}) async-start(), calls=%async_computation.22 | async-start | bytes 5898240 | tf_op jit(solution)/shard_map/reduce_scatter | solution.py:370
  449.5 6.6 collective-permute-start.7
  459.1 33.3 %all-to-all-start.3 = ((bf16[8,192,384]{2,1,0:T(8,128)(2,1)}), bf16[8,192,384]{2,1,0:T(8,128)(2,1)S(1)}, u32[]{:S(2)}, u32[]{:S(2)}) async-start(bf16[8,192,384]{2,1,0:T(8,128)(2,1)} %bitcast.47), calls=%async_computation.3 | async-start | bytes 2359296 | tf_op jit(solution)/shard_map/all_to_all | solution.py:262
  470.0 2.9 collective-permute-start.8
  492.4 32.6 %copy-start.10 = (bf16[8,192,384]{2,1,0:T(8,128)(2,1)}, bf16[8,192,384]{2,1,0:T(8,128)(2,1)S(1)}, u32[]{:S(2)}) copy-start(bf16[8,192,384]{2,1,0:T(8,128)(2,1)S(1)} %all-to-all-done.3) | copy-start | bytes 3538948
  525.0 36.5 %copy-start.63 = (f32[768]{0:T(1024)S(1)}, f32[768]{0:T(1024)}, u32[]{:S(2)}) copy-start(f32[768]{0:T(1024)} %get-tuple-element.103) | copy-start | bytes 9220
  525.0 36.5 %copy-start.75 = (bf16[768]{0:T(1024)(128)(2,1)S(1)}, bf16[768]{0:T(1024)(128)(2,1)}, u32[]{:S(2)}) copy-start(bf16[768]{0:T(1024)(128)(2,1)} %param.58) | copy-start | bytes 4612
  525.0 36.5 %copy-start.9 = (f32[672,768]{1,0:T(8,128)S(1)}, f32[672,768]{1,0:T(8,128)}, u32[]{:S(2)}) copy-start(f32[672,768]{1,0:T(8,128)} %copy-done.8) | copy-start | bytes 6193156
  525.0 32.1 %all-to-all-start.8 = ((bf16[8,96,768]{2,1,0:T(8,128)(2,1)}), bf16[8,96,768]{2,1,0:T(8,128)(2,1)}, u32[]{:S(2)}, u32[]{:S(2)}) async-start(bf16[8,96,768]{2,1,0:T(8,128)(2,1)} %bitcast.234), calls=%async_computation.11 | async-start | bytes 2359296 | tf_op jit(solution)/shard_map/all_to_all | solution.py:364
  557.2 32.5 %all-to-all-start.7 = ((bf16[8,96,768]{2,1,0:T(8,128)(2,1)}), bf16[8,96,768]{2,1,0:T(8,128)(2,1)}, u32[]{:S(2)}, u32[]{:S(2)}) async-start(bf16[8,96,768]{2,1,0:T(8,128)(2,1)} %bitcast.236), calls=%async_computation.9 | async-start | bytes 2359296 | tf_op jit(solution)/shard_map/all_to_all | solution.py:364
  561.4 191.0 %all-gather.21.cloned.1.call-start = ((), (), s32[]{:S(2)}) async-start(), calls=%async_computation.21 | async-start | bytes 1327104 | tf_op jit(solution)/shard_map/all_gather | solution.py:366
  589.6 44.6 %all-to-all-start.6 = ((bf16[8,96,768]{2,1,0:T(8,128)(2,1)}), bf16[8,96,768]{2,1,0:T(8,128)(2,1)}, u32[]{:S(2)}, u32[]{:S(2)}) async-start(bf16[8,96,768]{2,1,0:T(8,128)(2,1)} %bitcast.235), calls=%async_computation.7 | async-start | bytes 2359296 | tf_op jit(solution)/shard_map/all_to_all | solution.py:364
  593.9 162.0 %all-gather.19.cloned.1.call-start = ((), (), s32[]{:S(2)}) async-start(), calls=%async_computation.19 | async-start | bytes 1327104 | tf_op jit(solution)/shard_map/all_gather | solution.py:366
  600.0 6.6 collective-permute-start.6
  634.3 66.3 %all-to-all-start.5 = ((bf16[8,192,384]{2,1,0:T(8,128)(2,1)}), bf16[8,192,384]{2,1,0:T(8,128)(2,1)}, u32[]{:S(2)}, u32[]{:S(2)}) async-start(bf16[8,192,384]{2,1,0:T(8,128)(2,1)} %bitcast.207), calls=%async_computation.5 | async-start | bytes 2359296 | tf_op jit(solution)/shard_map/all_to_all | solution.py:262
  638.5 119.9 %all-gather.17.cloned.1.call-start = ((), (), s32[]{:S(2)}) async-start(), calls=%async_computation.17 | async-start | bytes 1327104 | tf_op jit(solution)/shard_map/all_gather | solution.py:366
  642.5 54.7 %copy-start.11 = (bf16[8,192,384]{2,1,0:T(8,128)(2,1)S(1)}, bf16[8,192,384]{2,1,0:T(8,128)(2,1)}, u32[]{:S(2)}) copy-start(bf16[8,192,384]{2,1,0:T(8,128)(2,1)} %copy-done.10) | copy-start | bytes 3538948
  700.6 43.2 %all-to-all-start.9 = ((bf16[8,96,768]{2,1,0:T(8,128)(2,1)}), bf16[8,96,768]{2,1,0:T(8,128)(2,1)S(1)}, u32[]{:S(2)}, u32[]{:S(2)}) async-start(bf16[8,96,768]{2,1,0:T(8,128)(2,1)} %bitcast.233), calls=%async_computation.13 | async-start | bytes 2359296 | tf_op jit(solution)/shard_map/all_to_all | solution.py:364
  706.3 84.3 %all-gather.23.cloned.1.call-start = ((), (), s32[]{:S(2)}) async-start(), calls=%async_computation.23 | async-start | bytes 1327104 | tf_op jit(solution)/shard_map/all_gather | solution.py:366
  708.0 16.3 %collective-permute-start.9 = (bf16[8,96,384]{2,1,0:T(8,128)(2,1)S(1)}, bf16[8,96,384]{2,1,0:T(8,128)(2,1)S(1)}, u32[]{:S(2)}, u32[]{:S(2)}) collective-permute-start(bf16[8,96,384]{2,1,0:T(8,128)(2,1)S(1)} %pad_maximum_fusion.19), channel_id=1, source_target_pairs={{0,2},{1,3},{2,0},{3,1},{4,6},{5,7},{6,4},{7,5},{8,10},{9,11},{10,... | collective-permute-start | bytes 1769480 | tf_op jit(solution)/shard_map/ppermute | solution.py:413
  709.1 27.8 %collective-permute-start.10 = (bf16[8,96,384]{2,1,0:T(8,128)(2,1)S(1)}, bf16[8,96,384]{2,1,0:T(8,128)(2,1)S(1)}, u32[]{:S(2)}, u32[]{:S(2)}) collective-permute-start(bf16[8,96,384]{2,1,0:T(8,128)(2,1)S(1)} %pad_maximum_fusion.20), channel_id=1, source_target_pairs={{0,2},{1,3},{2,0},{3,1},{4,6},{5,7},{6,4},{7,5},{8,10},{9,11},{10,... | collective-permute-start | bytes 1769480 | tf_op jit(solution)/shard_map/ppermute | solution.py:413
  713.2 33.2 %collective-permute-start.11 = (bf16[8,96,384]{2,1,0:T(8,128)(2,1)}, bf16[8,96,384]{2,1,0:T(8,128)(2,1)}, u32[]{:S(2)}, u32[]{:S(2)}) collective-permute-start(bf16[8,96,384]{2,1,0:T(8,128)(2,1)} %pad_maximum_fusion.21), channel_id=1, source_target_pairs={{0,2},{1,3},{2,0},{3,1},{4,6},{5,7},{6,4},{7,5},{8,10},{9,11},{10,... | collective-permute-start | bytes 1769480 | tf_op jit(solution)/shard_map/ppermute | solution.py:413
  (78 other events, 608.9 us)
Sparse Core Ops, SparseCore 0:
  10.2 42.6 all-gather.24
  55.0 58.3 all-gather.26
  115.0 37.4 all-gather.12
  153.9 37.4 all-gather.14
  280.9 47.1 reduce-scatter.8
  398.5 47.9 reduce-scatter.6
  449.7 47.8 reduce-scatter.4
  500.2 47.8 reduce-scatter.10
  579.5 54.3 all-gather.20
  636.5 48.6 all-gather.18
  700.7 47.8 all-gather.16
  750.6 39.9 all-gather.22
